TPU v7x, 32 devices: a whole 2x2x4 slice. The times are simulated.
32 devices in a mesh: shard: 4 (over x, core), rep: 8 (over z, y).
Axes of the slice: x: 2, y: 2, z: 4, core: 2. Of those that a mesh axis runs over, the one named last changes fastest.
Arguments:
- tokens: bfloat16 [8, 512, 1024], P('rep', 'shard'), may hold values from -6 to 6
- cotangent: bfloat16 [8, 512, 1024], P('rep', 'shard'), may hold values from -6 to 6
- segment_ids: int32 [8, 512], P('rep'), may hold values from 0 to 3, never falling along the last dimension, each value on 1 to 256 neighbouring positions
- intake: float32 [3, 1024, 1024], P(None, ('shard', 'rep')), may hold values from -0.1875 to 0.1875
- outlet: float32 [1024, 1024], P(('shard', 'rep')), may hold values from -1.5 to 1.5
- expand: float32 [4096, 1024], P(('shard', 'rep')), may hold values from -0.1875 to 0.1875
- shrink: float32 [4096, 1024], P(('shard', 'rep')), may hold values from -0.09375 to 0.09375
- affine: float32 [8, 1024], P(None, ('shard', 'rep')), may hold values from -0.8 to 0.8
- offset: float32 [4096], P(('shard', 'rep')), may hold values from -0.8 to 0.8
- intake_first: float32 [3, 1024, 1024], P(None, ('shard', 'rep')), may hold values from -15 to 15
- outlet_first: float32 [1024, 1024], P(('shard', 'rep')), may hold values from -15 to 15
- expand_first: float32 [4096, 1024], P(('shard', 'rep')), may hold values from -15 to 15
- shrink_first: float32 [4096, 1024], P(('shard', 'rep')), may hold values from -15 to 15
- affine_first: float32 [8, 1024], P(None, ('shard', 'rep')), may hold values from -15 to 15
- offset_first: float32 [4096], P(('shard', 'rep')), may hold values from -15 to 15
- intake_second: float32 [3, 1024, 1024], P(None, ('shard', 'rep')), may hold values from 1 to 100
- outlet_second: float32 [1024, 1024], P(('shard', 'rep')), may hold values from 1 to 100
- expand_second: float32 [4096, 1024], P(('shard', 'rep')), may hold values from 1 to 100
- shrink_second: float32 [4096, 1024], P(('shard', 'rep')), may hold values from 1 to 100
- affine_second: float32 [8, 1024], P(None, ('shard', 'rep')), may hold values from 1 to 100
- offset_second: float32 [4096], P(('shard', 'rep')), may hold values from 1 to 100
Outputs:
- layer_out: bfloat16 [8, 512, 1024], P('rep', 'shard')
- token_grad: bfloat16 [8, 512, 1024], P('rep', 'shard')
- intake_grad: float32 [3, 1024, 1024], P(None, ('shard', 'rep'))
- outlet_grad: float32 [1024, 1024], P(('shard', 'rep'))
- expand_grad: float32 [4096, 1024], P(('shard', 'rep'))
- shrink_grad: float32 [4096, 1024], P(('shard', 'rep'))
- affine_grad: float32 [8, 1024], P(None, ('shard', 'rep'))
- offset_grad: float32 [4096], P(('shard', 'rep'))
- intake_next: float32 [3, 1024, 1024], P(None, ('shard', 'rep'))
- outlet_next: float32 [1024, 1024], P(('shard', 'rep'))
- expand_next: float32 [4096, 1024], P(('shard', 'rep'))
- shrink_next: float32 [4096, 1024], P(('shard', 'rep'))
- affine_next: float32 [8, 1024], P(None, ('shard', 'rep'))
- offset_next: float32 [4096], P(('shard', 'rep'))
- intake_momentum: float32 [3, 1024, 1024], P(None, ('shard', 'rep'))
- outlet_momentum: float32 [1024, 1024], P(('shard', 'rep'))
- expand_momentum: float32 [4096, 1024], P(('shard', 'rep'))
- shrink_momentum: float32 [4096, 1024], P(('shard', 'rep'))
- affine_momentum: float32 [8, 1024], P(None, ('shard', 'rep'))
- offset_momentum: float32 [4096], P(('shard', 'rep'))
- intake_variance: float32 [3, 1024, 1024], P(None, ('shard', 'rep'))
- outlet_variance: float32 [1024, 1024], P(('shard', 'rep'))
- expand_variance: float32 [4096, 1024], P(('shard', 'rep'))
- shrink_variance: float32 [4096, 1024], P(('shard', 'rep'))
- affine_variance: float32 [8, 1024], P(None, ('shard', 'rep'))
- offset_variance: float32 [4096], P(('shard', 'rep'))
Inputs may be any that keep to these rules, and one draw needn't show every extreme that they name: `segment_ids`: within each sequence the numbers never fall along positions, every number appears, each document spans at most 256 positions and one spans exactly that many.
All inputs are finite; a program needn't handle non-finite values.
Results may differ from a plain program's by a relative error of at most 0.025.
Values may be sent and summed in bfloat16 or wider, within the bound.
No kernel may reach another device: no remote copies, remote signals or barrier semaphores. Data moves between devices by JAX's collectives and lax.ppermute only.
A program may use at most 128 MiB of HBM per device.

v0:
```python
import itertools
import math

import jax
import jax.numpy as jnp
from jax import lax
from jax.experimental import pallas as pl
from jax.experimental.pallas import tpu as pltpu
from jax.sharding import PartitionSpec as P


HEAD_DIM = 64


lr_rate = 0.03
beta_one = 0.9
beta_two = 0.95
adam_eps = 1e-08
weight_decay = 0.1
step_count = 3
norm_eps = 1e-05

f32 = jnp.float32
bf16 = jnp.bfloat16


def layer_norm(values_in):
    centred = values_in - jnp.mean(values_in, axis=-1, keepdims=True)
    inv_std = lax.rsqrt(jnp.mean(centred * centred, axis=-1, keepdims=True) + norm_eps)
    return (centred * inv_std, inv_std)


def norm_back(grad_normed, normed, inv_std):
    return inv_std * (
        grad_normed
        - jnp.mean(grad_normed, axis=-1, keepdims=True)
        - normed * jnp.mean(grad_normed * normed, axis=-1, keepdims=True)
    )


def adamw_step(weight, first_mom, second_mom, gradient):
    momentum = beta_one * first_mom + (1.0 - beta_one) * gradient
    variance = beta_two * second_mom + (1.0 - beta_two) * gradient * gradient
    fixed_mom = momentum / (1.0 - beta_one**step_count)
    fixed_var = variance / (1.0 - beta_two**step_count)
    return (
        weight - lr_rate * (fixed_mom / (jnp.sqrt(fixed_var) + adam_eps) + weight_decay * weight),
        momentum,
        variance,
    )


def dot_on(left_side, right_side, left_dim, right_dim):
    return lax.dot_general(
        left_side,
        right_side,
        (((left_dim,), (right_dim,)), ((), ())),
        preferred_element_type=f32,
    )


def dot_plain(left_side, right_side):
    return dot_on(left_side, right_side, 1, 0)


def dot_rows(left_side, right_side):
    return dot_on(left_side, right_side, 1, 1)


def dot_cols(left_side, right_side):
    return dot_on(left_side, right_side, 0, 0)


def masked_exp(query_head, key_head, same_doc):
    scores = dot_cols(key_head, query_head) * (1.0 / math.sqrt(HEAD_DIM))
    exp_scores = jnp.where(same_doc, jnp.exp(scores), 0.0)
    return exp_scores / jnp.sum(exp_scores, axis=0, keepdims=True)


def head_slices(head, heads, rows, stride, start):
    return [
        slice(base, base + rows)
        for base in range(head * stride + start, heads * stride * (HEAD_DIM // rows), heads * stride)
    ]


def read_head(ref, slices):
    return jnp.concatenate([ref[one, :] for one in slices], axis=0)


def write_head(ref, slices, value):
    rows = value.shape[0] // len(slices)
    for i, one in enumerate(slices):
        ref[one, :] = value[i * rows : (i + 1) * rows]


def fill(ref, pieces, start, stop):
    rows = stop - start
    for i, piece in enumerate(pieces):
        ref[i * rows : (i + 1) * rows, :] = piece[start:stop, :]


def split_out(far_ref, near_ref, make):
    half = near_ref.shape[0]
    far_ref[...] = make(slice(half, 2 * half)).astype(bf16)
    near_ref[...] = make(slice(0, half))


def attend_kernel(rows, in_rows, out_rows, unit_cols, count, *refs):
    pieces, refs = refs[:count], refs[count:]
    tokens, refs = refs[:-12], refs[-12:]
    picks_ref, seg_col_ref, seg_row_ref, *refs = refs
    w_in_ref, w_out_ref, group_ref, inner_ref, out_ref, coeff_ref, unit_ref, far_ref, near_ref = refs
    fill(w_in_ref, pieces, 0, in_rows)
    fill(w_out_ref, pieces, in_rows, in_rows + out_rows)
    fill(group_ref, tokens, 0, group_ref.shape[0] // len(tokens))
    small = [p[in_rows + out_rows :, :].astype(f32) for p in pieces]
    total = sum(small).astype(bf16)
    coeff_ref[...] = total
    unit_at = total.shape[0] // 2
    for i, one in enumerate(small):
        unit_ref[:, i * unit_cols : (i + 1) * unit_cols] = one[unit_at : unit_at + 1, :unit_cols]
    bias = dot_rows(picks_ref[...], total)
    product = dot_rows(w_in_ref[...], group_ref[...])
    heads = out_ref.shape[0] // HEAD_DIM
    blocks = HEAD_DIM // rows
    for slot in range(heads * blocks):
        base = slot * 3 * rows
        own = slice(slot * rows, (slot + 1) * rows)
        for i, add in enumerate((bias[own, 0:1], 0.0, bias[own, 1:2])):
            part = slice(base + i * rows, base + (i + 1) * rows)
            inner_ref[part, :] = (product[part] + add).astype(bf16)
    same_doc = seg_col_ref[...] == seg_row_ref[...]
    for head in range(heads):
        query, key, value = [
            read_head(inner_ref, head_slices(head, heads, rows, 3 * rows, i * rows))
            for i in range(3)
        ]
        probs = masked_exp(query, key, same_doc)
        attended = dot_plain(value, probs.astype(bf16)).astype(bf16)
        write_head(out_ref, head_slices(head, heads, rows, rows, 0), attended)
    split_out(far_ref, near_ref, lambda cols: dot_cols(out_ref[:, cols], w_out_ref[...]))


def units_kernel(start, stop, count, parts, *refs):
    pieces, refs = refs[:count], refs[count:]
    group, refs = refs[: -(parts + 4)], refs[-(parts + 4) :]
    unit_ref, w_ref, group_ref, slope_ref, *act_refs = refs
    fill(w_ref, pieces, start, stop)
    fill(group_ref, group, 0, group_ref.shape[0] // len(group))
    cols = act_refs[0].shape[1]
    for i, act_ref in enumerate(act_refs):
        own = slice(i * cols, (i + 1) * cols)
        hidden = dot_rows(group_ref[...], w_ref[own, :]) + unit_ref[:, own]
        bell = 0.5 * (1.0 + lax.erf(hidden * (1.0 / math.sqrt(2.0))))
        act_ref[...] = (hidden * bell).astype(bf16)
        slope = bell + hidden * jnp.exp(-0.5 * hidden * hidden) * (1.0 / math.sqrt(2.0 * math.pi))
        slope_ref[:, own] = slope


def shrink_kernel(count, *refs):
    pieces, refs = refs[:count], refs[count:]
    acts, (w_ref, far_ref, near_ref) = refs[:-3], refs[-3:]
    fill(w_ref, pieces, 0, pieces[0].shape[0])
    cols = acts[0].shape[1]

    def make(rows):
        terms = [
            dot_plain(act[rows, :], w_ref[i * cols : (i + 1) * cols, :])
            for i, act in enumerate(acts)
        ]
        return sum(terms[1:], terms[0])

    split_out(far_ref, near_ref, make)


def units_back_kernel(count, *refs):
    grads, refs = refs[:count], refs[count:]
    w_shrink_ref, w_expand_ref, slope_ref, group_ref, bias_ref, sum_ref, far_ref, near_ref = refs[:8]
    back_refs = refs[8:]
    fill(group_ref, grads, 0, grads[0].shape[0])
    cols = back_refs[0].shape[1]
    for i, back_ref in enumerate(back_refs):
        own = slice(i * cols, (i + 1) * cols)
        back = dot_rows(group_ref[...], w_shrink_ref[own, :]) * slope_ref[:, own]
        back_ref[...] = back.astype(bf16)
        sum_ref[:, own] = jnp.sum(back, axis=0, keepdims=True)

    def make(rows):
        terms = [
            dot_plain(back[rows, :], w_expand_ref[i * cols : (i + 1) * cols, :])
            for i, back in enumerate(back_refs)
        ]
        return sum(terms[1:], terms[0])

    split_out(far_ref, near_ref, make)
    bias_ref[...] = jnp.sum(group_ref[...].astype(f32), axis=0, keepdims=True)


def attend_back_kernel(rows, count, *refs):
    grads, refs = refs[:count], refs[count:]
    inner_ref, w_in_ref, w_out_ref, seg_col_ref, seg_row_ref = refs[:5]
    group_ref, shared_ref, out_ref, sum_ref, far_ref, near_ref, grad_ref = refs[5:]
    score_scale = 1.0 / math.sqrt(HEAD_DIM)
    own_rows = group_ref.shape[0] // count
    fill(group_ref, grads, 0, own_rows)
    grad_ref[...] = dot_rows(w_out_ref[...], group_ref[...]).astype(bf16)
    heads = grad_ref.shape[0] // HEAD_DIM
    same_doc = seg_col_ref[...] == seg_row_ref[...]
    for head in range(heads):
        slots = [head_slices(head, heads, rows, 3 * rows, i * rows) for i in range(3)]
        query, key, value = [read_head(inner_ref, one) for one in slots]
        outer = head_slices(head, heads, rows, rows, 0)
        grad = read_head(grad_ref, outer)
        probs = masked_exp(query, key, same_doc)
        prob_grad = dot_cols(value, grad)
        row_dots = jnp.sum(probs * prob_grad, axis=0, keepdims=True)
        score_half = (probs * (prob_grad - row_dots)).astype(bf16)
        dq = dot_plain(key, score_half) * score_scale
        dk = dot_rows(query, score_half) * score_scale
        dv = dot_rows(grad, probs.astype(bf16))
        for one, value_out in zip(slots, (dq, dk, dv)):
            write_head(out_ref, one, value_out.astype(bf16))
        for column, value_out in enumerate((dq, dv)):
            sums = jnp.sum(value_out, axis=1, keepdims=True)
            for i, one in enumerate(outer):
                sum_ref[one, column : column + 1] = sums[i * rows : (i + 1) * rows]
    split_out(far_ref, near_ref, lambda cols: dot_cols(out_ref[:, cols], w_in_ref[...]))
    bias = jnp.sum(group_ref[...].astype(f32), axis=0, keepdims=True)
    shared_ref[...] = sum(g[own_rows:, :].astype(f32) for g in grads)
    shared_ref[shared_ref.shape[0] - 1 :, :] = bias


def factor_rep(count, first):
    factors = [first]
    count //= first
    while count > 1:
        step = 4 if count % 4 == 0 else 2
        factors.append(step)
        count //= step
    return factors


def make_body(groups, replicas):
    shard_bits = [1 << i for i in range(groups.bit_length() - 1)]

    def swap(value, bit):
        return lax.ppermute(value, "shard", [(i, i ^ bit) for i in range(groups)])

    slot_order = sorted(range(groups), key=lambda i: (i & 1, i))

    def gather_group(piece):
        pieces = {0: piece}
        for bit in reversed(shard_bits):
            for slot in list(pieces):
                pieces[slot ^ bit] = swap(pieces[slot], bit)
        return [pieces[i] for i in slot_order]

    def scatter_group(near, far):
        total = near + swap(far, 1).astype(f32)
        for bit in reversed(shard_bits[1:]):
            half = total.shape[0] // 2
            came = swap(total[half:].astype(bf16), bit)
            total = total[:half] + came.astype(f32)
        return total

    def body(
        tokens,
        cotangent,
        segment_ids,
        intake,
        outlet,
        expand,
        shrink,
        affine,
        offset,
        intake_first,
        outlet_first,
        expand_first,
        shrink_first,
        affine_first,
        offset_first,
        intake_second,
        outlet_second,
        expand_second,
        shrink_second,
        affine_second,
        offset_second,
    ):
        own_rows = tokens.shape[1]
        width = tokens.shape[2]
        seq_len = own_rows * groups
        head_cols = intake.shape[1] * replicas
        factors = factor_rep(replicas, head_cols // HEAD_DIM)
        strides = [math.prod(factors[i + 1 :]) for i in range(len(factors))]
        lead = factors[0]
        suffixes = list(itertools.product(*[range(f) for f in factors[1:]]))
        own_shard = lax.axis_index("shard")
        own_rep = lax.axis_index("rep")

        bulk = len(factors) > 2
        aligned = intake.shape[1] % 16 == 0
        head_rows = intake.shape[1] if aligned else HEAD_DIM

        def shift(value, level, amount):
            pairs = []
            for r in range(replicas):
                coord = (r // strides[level]) % factors[level]
                moved = (coord + amount) % factors[level]
                pairs.append((r, r + (moved - coord) * strides[level]))
            return lax.ppermute(value, "rep", pairs)

        def gather_rep(piece):
            parts = [piece] + [shift(piece, 0, k) for k in range(1, lead)]
            if bulk:
                return gather_rest({(): jnp.concatenate(parts, axis=0)})
            blocks = list(parts)
            for k in range(1, len(suffixes)):
                blocks += [shift(v, 1, k) for v in parts]
            return blocks

        def gather_rest(blocks):
            for level in range(1, len(factors)):
                joined = jnp.concatenate(list(blocks.values()), axis=0)
                grown = {s + (0,): v for s, v in blocks.items()}
                for k in range(1, factors[level]):
                    came = jnp.split(shift(joined, level, k), len(blocks))
                    grown.update({s + (k,): v for s, v in zip(blocks, came)})
                blocks = grown
            return [p for s in suffixes for p in jnp.split(blocks[s], lead)]

        def join(pieces, start, stop):
            return jnp.concatenate([p[start:stop] for p in pieces], axis=0)

        def order_heads(joined, kinds):
            split = joined.reshape(len(suffixes), lead, kinds, -1, joined.shape[1])
            return split.transpose(1, 2, 0, 3, 4).reshape(joined.shape)

        def by_suffix(left_side, right_side, kinds, parts):
            if aligned:
                count = len(suffixes) * parts
                rows = left_side.shape[0] // count
                products = [
                    dot_plain(left_side[i * rows : (i + 1) * rows], right_side)
                    for i in range(count)
                ]
                return [products[i * parts : (i + 1) * parts] for i in range(len(suffixes))]
            product = dot_plain(left_side, right_side)
            split = product.reshape(lead, kinds, len(suffixes), -1, product.shape[1])
            split = split.transpose(2, 0, 1, 3, 4)
            return [[p] for p in split.reshape(len(suffixes), -1, product.shape[1])]

        def scatter_rep(blocks, shared=None, units=None):
            if bulk:
                blocks = [[jnp.concatenate(parts, axis=0)] for parts in blocks]
            blocks = dict(zip(suffixes, blocks))
            units = {} if shared is None else dict(zip(suffixes, units))

            def pack(pieces, line):
                if line is None:
                    return jnp.concatenate([p.astype(bf16) for p in pieces], axis=0)
                line = jnp.pad(line, ((0, extra - small_rows - 1), (0, width - line.shape[1])))
                joined = [p.astype(bf16) for p in [*pieces, shared, line]]
                return jnp.concatenate(joined, axis=0)

            for level in reversed(range(1, len(factors))):
                merged = {s[:-1]: list(v) for s, v in blocks.items() if s[-1] == 0}
                lines = {s[:-1]: v for s, v in units.items() if s[-1] == 0}
                total = shared
                for k in range(1, factors[level]):
                    for part in reversed(range(len(next(iter(merged.values()))))):
                        line = None
                        if shared is not None and part == 0:
                            line = jnp.concatenate([units[s + (k,)] for s in merged], axis=1)
                        sent = pack([blocks[s + (k,)][part] for s in merged], line)
                        came = shift(sent, level, -k).astype(f32)
                        rows = blocks[next(iter(blocks))][part].shape[0]
                        for i, s in enumerate(merged):
                            merged[s][part] = merged[s][part] + came[i * rows : (i + 1) * rows]
                        if line is not None:
                            at = came.shape[0] - extra
                            total = total + came[at : at + small_rows]
                            size = line.shape[1] // len(merged)
                            row = came[at + small_rows][None]
                            for i, s in enumerate(merged):
                                lines[s] = lines[s] + row[:, i * size : (i + 1) * size]
                blocks, shared, units = merged, total, lines
            parts = blocks[()]
            per_part = lead // len(parts)
            rows = parts[0].shape[0] // per_part

            def slot(k):
                at = k % per_part * rows
                return parts[k // per_part][at : at + rows]

            result, total = slot(0), shared
            if shared is not None:
                size = units[()].shape[1] // lead
                line_total = units[()][:, :size]
            for k in range(1, lead):
                line = None if shared is None else units[()][:, k * size : (k + 1) * size]
                came = shift(pack([slot(k)], line), 0, -k).astype(f32)
                result = result + came[:rows]
                if shared is not None:
                    total = total + came[rows : rows + small_rows]
                    line_total = line_total + came[rows + small_rows][None, :size]
            return result if shared is None else (result, total, line_total)

        extra = 16
        own_cols = affine.shape[1]
        own_start = (own_shard * replicas + own_rep) * own_cols
        small_rows = affine.shape[0]
        placed = lax.dynamic_update_slice(
            jnp.zeros((small_rows, width), bf16), affine.astype(bf16), (0, own_start)
        )
        unit_row = jnp.pad(
            offset.astype(bf16).reshape(1, -1),
            ((0, extra - small_rows - 1), (0, width - offset.shape[0])),
        )
        source = tokens.reshape(own_rows, width)
        own_small = jnp.pad(placed, ((0, extra - small_rows), (0, 0)))
        token_parts = gather_group(jnp.concatenate([source, own_small], axis=0))

        intake_low = intake.astype(bf16).reshape(-1, width)
        in_rows = intake_low.shape[0]
        out_rows = outlet.shape[0]
        wide_rows = expand.shape[0]
        pieces = gather_rep(
            jnp.concatenate([intake_low, outlet.astype(bf16), placed, unit_row], axis=0)
        )
        placed_group = sum(p[own_rows:].astype(f32) for p in token_parts).astype(bf16)
        wide_pieces = gather_rep(jnp.concatenate([expand.astype(bf16), placed_group], axis=0))
        shrink_pieces = gather_rep(shrink.astype(bf16))
        unit_cols = offset.shape[0]
        if not aligned:
            at = in_rows + out_rows
            line = jnp.concatenate([p[at + small_rows :][:1, :unit_cols] for p in pieces], axis=1)
            line = jnp.pad(line, ((0, extra - small_rows - 1), (0, width - line.shape[1])))
            placed_all = sum(p[at : at + small_rows].astype(f32) for p in pieces).astype(bf16)
            w_in = order_heads(join(pieces, 0, in_rows), 3)
            w_out = order_heads(join(pieces, in_rows, at), 1)
            pieces = [jnp.concatenate([w_in, w_out, placed_all, line], axis=0)]
            wide_joined = join(wide_pieces, 0, wide_rows)
            placed_all = sum(p[wide_rows:].astype(f32) for p in wide_pieces).astype(bf16)
            wide_pieces = [jnp.concatenate([wide_joined, placed_all], axis=0)]
            shrink_pieces = [join(shrink_pieces, 0, wide_rows)]
            in_rows, out_rows = in_rows * replicas, out_rows * replicas
            wide_rows, unit_cols = wide_rows * replicas, unit_cols * replicas
        coeffs = sum(p[wide_rows : wide_rows + small_rows].astype(f32) for p in wide_pieces)
        units = wide_rows * len(wide_pieces)

        index = lax.broadcasted_iota(jnp.int32, (head_cols, 1), 0)
        part_rows = intake.shape[1]
        if aligned:
            suffix_index = index // (lead * part_rows)
            lead_index = index // part_rows % lead
        else:
            lead_index = index // HEAD_DIM
            suffix_index = index // part_rows % len(suffixes)
        slot_index = lead_index * len(suffixes) + suffix_index
        feature_rep = jnp.zeros_like(index)
        for stride, factor in zip(strides, factors):
            slot_at = (slot_index // stride) % factor
            coord = (own_rep // stride) % factor
            feature_rep = feature_rep + ((coord - slot_at + factor) % factor) * stride
        feature = (own_shard * replicas + feature_rep) * own_cols + index % own_cols
        picks = feature == lax.broadcasted_iota(jnp.int32, (head_cols, width), 1)

        every_seg = segment_ids.reshape(seq_len)
        seg_slots = jnp.concatenate(
            [
                lax.dynamic_slice_in_dim(every_seg, (own_shard ^ k) * own_rows, own_rows)
                for k in slot_order
            ]
        )
        seg_col = seg_slots.reshape(seq_len, 1)
        seg_row = seg_slots.reshape(1, seq_len)

        def call(kernel, outs, *operands, scratch=()):
            return pl.pallas_call(
                kernel,
                out_shape=[jax.ShapeDtypeStruct(shape, dtype) for shape, dtype in outs],
                scratch_shapes=[pltpu.VMEM(shape, dtype) for shape, dtype in scratch],
            )(*operands)

        half = seq_len // 2
        full = (seq_len, width)
        two_halves = [((half, width), bf16), ((half, width), f32)]
        w_in, w_out, group_tokens, inner, attended, _, unit_bias, far, near = call(
            lambda *refs: attend_kernel(head_rows, in_rows, out_rows, unit_cols, len(pieces), *refs),
            [
                ((3 * head_cols, width), bf16),
                ((head_cols, width), bf16),
                (full, bf16),
                ((3 * head_cols, seq_len), bf16),
                ((head_cols, seq_len), bf16),
                ((extra, width), bf16),
                ((1, units), f32),
                *two_halves,
            ],
            *pieces,
            *token_parts,
            picks.astype(bf16),
            seg_col,
            seg_row,
        )
        attn_out = scatter_group(near, far)
        resid_one = source.astype(f32) + attn_out + coeffs[2]
        normed_one, inv_one = layer_norm(resid_one)
        mixed_one = normed_one * (1.0 + coeffs[3]) + coeffs[4]
        inner_parts = gather_group(mixed_one.astype(bf16))
        parts = 2
        count = parts * (1 if bulk else len(suffixes))
        thin = [((seq_len, units // count), bf16)] * count
        w_expand, group_in, slope, *acts = call(
            lambda *refs: units_kernel(0, wide_rows, len(wide_pieces), count, *refs),
            [((units, width), bf16), (full, bf16), ((seq_len, units), f32), *thin],
            *wide_pieces,
            *inner_parts,
            unit_bias,
        )
        w_shrink, far, near = call(
            lambda *refs: shrink_kernel(len(shrink_pieces), *refs),
            [((units, width), bf16), *two_halves],
            *shrink_pieces,
            *acts,
        )
        ffn_out = scatter_group(near, far)
        resid_two = mixed_one + ffn_out + coeffs[5]
        normed_two, inv_two = layer_norm(resid_two)
        layer_out = (normed_two * (1.0 + coeffs[6]) + coeffs[7]).astype(bf16)

        out_grad = cotangent.reshape(own_rows, width).astype(f32)
        grad_two = norm_back(out_grad * (1.0 + coeffs[6]), normed_two, inv_two)
        grad_parts = gather_group(grad_two.astype(bf16))
        gain_two = jnp.sum(out_grad * normed_two, axis=0)
        shift_two = jnp.sum(out_grad, axis=0)
        group_grad, bias_two, unit_sums, far, near, *backs = call(
            lambda *refs: units_back_kernel(groups, *refs),
            [(full, bf16), ((1, width), f32), ((1, units), f32), *two_halves, *thin],
            *grad_parts,
            w_shrink,
            w_expand,
            slope,
        )

        def unit_blocks(lefts, right_side):
            if bulk:
                product = dot_cols(jnp.concatenate(lefts, axis=1), right_side)
                return [[p] for p in jnp.split(product, len(suffixes))]
            products = [dot_cols(left, right_side) for left in lefts]
            return [products[i * parts : (i + 1) * parts] for i in range(len(suffixes))]

        shrink_grad = scatter_rep(unit_blocks(acts, group_grad))
        grad_inner = scatter_group(near, far)
        expand_grad = scatter_rep(unit_blocks(backs, group_in))
        grad_mixed = grad_two + grad_inner
        grad_one = norm_back(grad_mixed * (1.0 + coeffs[3]), normed_one, inv_one)
        gain_one = jnp.sum(grad_mixed * normed_one, axis=0)
        shift_one = jnp.sum(grad_mixed, axis=0)
        sums = jnp.stack([gain_one, shift_one, gain_two, shift_two])
        sums = jnp.pad(sums, ((0, extra - sums.shape[0]), (0, 0)))
        one_parts = gather_group(
            jnp.concatenate([grad_one.astype(bf16), sums.astype(bf16)], axis=0)
        )
        group_one, sums, inner_grad, head_sums, far, near = call(
            lambda *refs: attend_back_kernel(head_rows, groups, *refs),
            [
                (full, bf16),
                ((extra, width), f32),
                (inner.shape, bf16),
                ((head_cols, 2), f32),
                *two_halves,
            ],
            *one_parts,
            inner,
            w_in,
            w_out,
            seg_col,
            seg_row,
            scratch=[((head_cols, seq_len), bf16)],
        )
        token_grad = (grad_one + scatter_group(near, far)).astype(bf16)
        outlet_grad = scatter_rep(by_suffix(attended, group_one, 1, 1))
        bias_rows = lax.dot_general(
            head_sums,
            picks.astype(f32),
            (((0,), (0,)), ((), ())),
            precision=lax.Precision.HIGHEST,
            preferred_element_type=f32,
        )
        shared = jnp.concatenate(
            [bias_rows, sums[extra - 1 :], sums[0:2], bias_two, sums[2:4]], axis=0
        )
        intake_grad, affine_full, offset_grad = scatter_rep(
            by_suffix(inner_grad, group_tokens, 3, parts),
            shared,
            jnp.split(unit_sums, len(suffixes), axis=1),
        )
        intake_grad = intake_grad.reshape(intake.shape)
        offset_grad = offset_grad.reshape(offset.shape)
        affine_grad = lax.dynamic_slice(affine_full, (0, own_start), affine.shape)

        intake_next, intake_momentum, intake_variance = adamw_step(
            intake, intake_first, intake_second, intake_grad
        )
        outlet_next, outlet_momentum, outlet_variance = adamw_step(
            outlet, outlet_first, outlet_second, outlet_grad
        )
        expand_next, expand_momentum, expand_variance = adamw_step(
            expand, expand_first, expand_second, expand_grad
        )
        shrink_next, shrink_momentum, shrink_variance = adamw_step(
            shrink, shrink_first, shrink_second, shrink_grad
        )
        affine_next, affine_momentum, affine_variance = adamw_step(
            affine, affine_first, affine_second, affine_grad
        )
        offset_next, offset_momentum, offset_variance = adamw_step(
            offset, offset_first, offset_second, offset_grad
        )
        return (
            layer_out.reshape(tokens.shape),
            token_grad.reshape(cotangent.shape),
            intake_grad,
            outlet_grad,
            expand_grad,
            shrink_grad,
            affine_grad,
            offset_grad,
            intake_next,
            outlet_next,
            expand_next,
            shrink_next,
            affine_next,
            offset_next,
            intake_momentum,
            outlet_momentum,
            expand_momentum,
            shrink_momentum,
            affine_momentum,
            offset_momentum,
            intake_variance,
            outlet_variance,
            expand_variance,
            shrink_variance,
            affine_variance,
            offset_variance,
        )

    return body


def solution(mesh):
    rows = P("rep", "shard", None)
    params = (
        P(None, ("shard", "rep"), None),
        P(("shard", "rep"), None),
        P(("shard", "rep"), None),
        P(("shard", "rep"), None),
        P(None, ("shard", "rep")),
        P(("shard", "rep")),
    )
    body = make_body(mesh.shape["shard"], mesh.shape["rep"])

    return jax.shard_map(
        body,
        mesh=mesh,
        in_specs=(rows, rows, P("rep", None)) + params * 3,
        out_specs=(rows, rows) + params * 4,
        check_vma=False,
    )
```

profile of v0, /device:TPU:0, one launch (start us, length us, event | category | flops | bytes accessed | tf_op | source)
XLA Modules:
  0.0 324.5 jit_solution(1594061987406193570)
XLA Ops:
  17.4 11.8 %collective-permute-done.1.refs_2_ = bf16[144,1024]{1,0:T(8,128)(2,1)S(1)} collective-permute-done((bf16[144,1024]{1,0:T(8,128)(2,1)S(1)}, bf16[144,1024]{1,0:T(8,128)(2,1)S(1)}, u32[]{:S(2)}, u32[]{:S(2)}) %collective-permute-start.1) | collective-permute-done | bytes 294944 | tf_op jit(solution)/shard_map/ppermute | solution.py:311
  33.8 5.3 %collective-permute-done.4.refs_5_ = bf16[144,1024]{1,0:T(8,128)(2,1)S(1)} collective-permute-done((bf16[144,1024]{1,0:T(8,128)(2,1)S(1)}, bf16[144,1024]{1,0:T(8,128)(2,1)S(1)}, u32[]{:S(2)}, u32[]{:S(2)}) %collective-permute-start.4) | collective-permute-done | bytes 294944 | tf_op jit(solution)/shard_map/ppermute | solution.py:311
  39.1 6.3 %collective-permute-done.5.refs_6_ = bf16[144,1024]{1,0:T(8,128)(2,1)S(1)} collective-permute-done((bf16[144,1024]{1,0:T(8,128)(2,1)S(1)}, bf16[144,1024]{1,0:T(8,128)(2,1)S(1)}, u32[]{:S(2)}, u32[]{:S(2)}) %collective-permute-start.5) | collective-permute-done | bytes 294944 | tf_op jit(solution)/shard_map/ppermute | solution.py:311
  45.4 5.3 %collective-permute-done.6.refs_7_ = bf16[144,1024]{1,0:T(8,128)(2,1)S(1)} collective-permute-done((bf16[144,1024]{1,0:T(8,128)(2,1)S(1)}, bf16[144,1024]{1,0:T(8,128)(2,1)S(1)}, u32[]{:S(2)}, u32[]{:S(2)}) %collective-permute-start.6) | collective-permute-done | bytes 294944 | tf_op jit(solution)/shard_map/ppermute | solution.py:311
  52.1 7.3 %shard_map.404 = (bf16[768,1024]{1,0:T(8,128)(2,1)}, bf16[256,1024]{1,0:T(8,128)(2,1)}, bf16[512,1024]{1,0:T(8,128)(2,1)}, bf16[768,512]{1,0:T(8,128)(2,1)}, bf1...) custom-call(bf16[144,1024]{1,0:T(8,128)(2,1)} %copy-done.12, ...), custom_call_target="tpu_custom_call" | custom-call | tf_op jit(solution)/shard_map/pallas_call | solution.py:480
  69.4 5.8 %collective-permute-done.12.refs_1_ = bf16[144,1024]{1,0:T(8,128)(2,1)S(1)} collective-permute-done((bf16[144,1024]{1,0:T(8,128)(2,1)S(1)}, bf16[144,1024]{1,0:T(8,128)(2,1)S(1)}, u32[]{:S(2)}, u32[]{:S(2)}) %collective-permute-start.12) | collective-permute-done | bytes 294944 | tf_op jit(solution)/shard_map/ppermute | solution.py:311
  76.9 10.7 %collective-permute-done.13.refs_2_ = bf16[144,1024]{1,0:T(8,128)(2,1)S(1)} collective-permute-done((bf16[144,1024]{1,0:T(8,128)(2,1)S(1)}, bf16[144,1024]{1,0:T(8,128)(2,1)S(1)}, u32[]{:S(2)}, u32[]{:S(2)}) %collective-permute-start.13) | collective-permute-done | bytes 294944 | tf_op jit(solution)/shard_map/ppermute | solution.py:311
  89.7 6.5 %collective-permute-start.19 = (bf16[128,1024]{1,0:T(8,128)(2,1)S(1)}, bf16[128,1024]{1,0:T(8,128)(2,1)S(1)}, u32[]{:S(2)}, u32[]{:S(2)}) collective-permute-start(bf16[128,1024]{1,0:T(8,128)(2,1)S(1)} %convert_element_type.250.refs_0_), channel_id=1, source_target_pairs={{0,2},{1,3},{2,4},{3,5},{4,6},{5,7},{6,0},{7,1},{8,10},{9,11},{10,... | collective-permute-start | bytes 786440 | tf_op jit(solution)/shard_map/ppermute | solution.py:311
  106.4 4.9 %collective-permute-start.21 = (bf16[128,1024]{1,0:T(8,128)(2,1)S(1)}, bf16[128,1024]{1,0:T(8,128)(2,1)S(1)}, u32[]{:S(2)}, u32[]{:S(2)}) collective-permute-start(bf16[128,1024]{1,0:T(8,128)(2,1)S(1)} %convert_element_type.250.refs_0_), channel_id=1, source_target_pairs={{0,6},{1,7},{2,0},{3,1},{4,2},{5,3},{6,4},{7,5},{8,14},{9,15},{10,... | collective-permute-start | bytes 786440 | tf_op jit(solution)/shard_map/ppermute | solution.py:311
  113.2 8.8 %collective-permute-done.20.refs_2_ = bf16[128,1024]{1,0:T(8,128)(2,1)S(1)} collective-permute-done((bf16[128,1024]{1,0:T(8,128)(2,1)S(1)}, bf16[128,1024]{1,0:T(8,128)(2,1)S(1)}, u32[]{:S(2)}, u32[]{:S(2)}) %collective-permute-start.20) | collective-permute-done | bytes 262176 | tf_op jit(solution)/shard_map/ppermute | solution.py:311
  125.8 5.5 %shard_map.405 = (bf16[1024,1024]{1,0:T(8,128)(2,1)}, bf16[512,1024]{1,0:T(8,128)(2,1)}, f32[512,1024]{1,0:T(8,128)}, bf16[512,256]{1,0:T(8,128)(2,1)}, bf16[512...) custom-call(bf16[144,1024]{1,0:T(8,128)(2,1)} %copy-done.9, bf16[144,1024]{1,0:T(8,128)(2,1)} %copy-done.35, ...), custom_call_target="tpu_custom_call" | custom-call | tf_op jit(solution)/shard_map/pallas_call | solution.py:480
  145.4 7.8 %collective-permute-done.30 = bf16[128,1024]{1,0:T(8,128)(2,1)S(1)} collective-permute-done((bf16[128,1024]{1,0:T(8,128)(2,1)S(1)}, bf16[128,1024]{1,0:T(8,128)(2,1)S(1)}, u32[]{:S(2)}, u32[]{:S(2)}) %collective-permute-start.30) | collective-permute-done | bytes 262176 | tf_op jit(solution)/shard_map/ppermute | solution.py:248
  154.9 6.9 %collective-permute-done.31.refs_1_ = bf16[128,1024]{1,0:T(8,128)(2,1)S(1)} collective-permute-done((bf16[128,1024]{1,0:T(8,128)(2,1)S(1)}, bf16[128,1024]{1,0:T(8,128)(2,1)S(1)}, u32[]{:S(2)}, u32[]{:S(2)}) %collective-permute-start.31) | collective-permute-done | bytes 262176 | tf_op jit(solution)/shard_map/ppermute | solution.py:248
  164.1 6.8 %shard_map.407 = (bf16[512,1024]{1,0:T(8,128)(2,1)}, f32[1,1024]{1,0:T(1,128)}, f32[1,1024]{1,0:T(1,128)}, bf16[256,1024]{1,0:T(8,128)(2,1)}, f32[256,1024]{1,0:...) custom-call(bf16[128,1024]{1,0:T(8,128)(2,1)} %copy-done.20, ...), custom_call_target="tpu_custom_call" | custom-call | tf_op jit(solution)/shard_map/pallas_call | solution.py:480
  181.4 8.8 %collective-permute-done.55 = bf16[256,1024]{1,0:T(8,128)(2,1)S(1)} collective-permute-done((bf16[256,1024]{1,0:T(8,128)(2,1)S(1)}, bf16[256,1024]{1,0:T(8,128)(2,1)S(1)}, u32[]{:S(2)}, u32[]{:S(2)}) %collective-permute-start.55) | collective-permute-done | bytes 524320 | tf_op jit(solution)/shard_map/ppermute | solution.py:311
  190.7 8.8 %collective-permute-start.56 = (bf16[128,1024]{1,0:T(8,128)(2,1)S(1)}, bf16[128,1024]{1,0:T(8,128)(2,1)S(1)}, u32[]{:S(2)}, u32[]{:S(2)}) collective-permute-start(bf16[128,1024]{1,0:T(8,128)(2,1)S(1)} %slice.441), channel_id=1, source_target_pairs={{0,6},{1,7},{2,0},{3,1},{4,2},{5,3},{6,4},{7,5},{8,14},{9,15},{10,... | collective-permute-start | bytes 786440 | tf_op jit(solution)/shard_map/ppermute | solution.py:311
  204.1 8.6 %collective-permute-done.50 = bf16[256,1024]{1,0:T(8,128)(2,1)S(1)} collective-permute-done((bf16[256,1024]{1,0:T(8,128)(2,1)S(1)}, bf16[256,1024]{1,0:T(8,128)(2,1)S(1)}, u32[]{:S(2)}, u32[]{:S(2)}) %collective-permute-start.50) | collective-permute-done | bytes 524320 | tf_op jit(solution)/shard_map/ppermute | solution.py:311
  212.6 6.0 %collective-permute-start.59 = (bf16[128,1024]{1,0:T(8,128)(2,1)S(1)}, bf16[128,1024]{1,0:T(8,128)(2,1)S(1)}, u32[]{:S(2)}, u32[]{:S(2)}) collective-permute-start(bf16[128,1024]{1,0:T(8,128)(2,1)S(1)} %get-tuple-element.135), channel_id=1, source_target_pairs={{0,2},{1,3},{2,4},{3,5},{4,6},{5,7},{6,0},{7,1},{8,10},{9,11},{10,... | collective-permute-start | bytes 786440 | tf_op jit(solution)/shard_map/ppermute | solution.py:311
  223.3 8.8 %collective-permute-start.51 = (bf16[128,1024]{1,0:T(8,128)(2,1)S(1)}, bf16[128,1024]{1,0:T(8,128)(2,1)S(1)}, u32[]{:S(2)}, u32[]{:S(2)}) collective-permute-start(bf16[128,1024]{1,0:T(8,128)(2,1)S(1)} %slice.442), channel_id=1, source_target_pairs={{0,6},{1,7},{2,0},{3,1},{4,2},{5,3},{6,4},{7,5},{8,14},{9,15},{10,... | collective-permute-start | bytes 786440 | tf_op jit(solution)/shard_map/ppermute | solution.py:311
  237.2 5.8 %collective-permute-done.36.refs_1_ = bf16[144,1024]{1,0:T(8,128)(2,1)S(1)} collective-permute-done((bf16[144,1024]{1,0:T(8,128)(2,1)S(1)}, bf16[144,1024]{1,0:T(8,128)(2,1)S(1)}, u32[]{:S(2)}, u32[]{:S(2)}) %collective-permute-start.36) | collective-permute-done | bytes 294944 | tf_op jit(solution)/shard_map/ppermute | solution.py:248
  243.0 10.2 %collective-permute-done.53 = bf16[128,1024]{1,0:T(8,128)(2,1)S(1)} collective-permute-done((bf16[128,1024]{1,0:T(8,128)(2,1)S(1)}, bf16[128,1024]{1,0:T(8,128)(2,1)S(1)}, u32[]{:S(2)}, u32[]{:S(2)}) %collective-permute-start.53) | collective-permute-done | bytes 262176 | tf_op jit(solution)/shard_map/ppermute | solution.py:311
  255.6 9.0 %shard_map.408 = (bf16[512,1024]{1,0:T(8,128)(2,1)}, f32[16,1024]{1,0:T(8,128)}, bf16[768,512]{1,0:T(8,128)(2,1)}, f32[256,2]{1,0:T(8,128)}, bf16[256,1024]{1,0:T(8,128)(2,1)}, /*index=5*/f32[256,1024]{1,0:T(8,128)}) custom-call(bf16[144,1024]{1,0:T(8,128)(2,1)} %copy-done.11, bf16[144,1024]{1,0:T(8,128)(2,1)} %copy-done.47, bf16[144,1024]{1,0:T(8,128)(2,1)} %copy-done.49, ...), custom_call_target="tpu_custom_call" | custom-call | tf_op jit(solution)/shard_map/pallas_call | solution.py:480
  272.9 10.4 %collective-permute-done.46 = bf16[128,1024]{1,0:T(8,128)(2,1)S(1)} collective-permute-done((bf16[128,1024]{1,0:T(8,128)(2,1)S(1)}, bf16[128,1024]{1,0:T(8,128)(2,1)S(1)}, u32[]{:S(2)}, u32[]{:S(2)}) %collective-permute-start.46) | collective-permute-done | bytes 262176 | tf_op jit(solution)/shard_map/ppermute | solution.py:311
  309.1 11.8 %collective-permute-done.44 = bf16[112,1024]{1,0:T(8,128)(2,1)S(1)} collective-permute-done((bf16[112,1024]{1,0:T(8,128)(2,1)S(1)}, bf16[112,1024]{1,0:T(8,128)(2,1)S(1)}, u32[]{:S(2)}, u32[]{:S(2)}) %collective-permute-start.44) | collective-permute-done | bytes 229408 | tf_op jit(solution)/shard_map/ppermute | solution.py:311
  (383 shorter events, 134.5 us)
Async XLA Ops:
  7.4 21.8 %collective-permute-start.1 = (bf16[144,1024]{1,0:T(8,128)(2,1)S(1)}, bf16[144,1024]{1,0:T(8,128)(2,1)S(1)}, u32[]{:S(2)}, u32[]{:S(2)}) collective-permute-start(bf16[144,1024]{1,0:T(8,128)(2,1)S(1)} %fusion.34.refs_0_), channel_id=1, source_target_pairs={{0,4},{1,5},{2,6},{3,7},{4,0},{5,1},{6,2},{7,3},{8,12},{9,13},{10,... | collective-permute-start | bytes 884744 | tf_op jit(solution)/shard_map/ppermute | solution.py:311
  10.0 20.7 %collective-permute-start.2 = (bf16[144,1024]{1,0:T(8,128)(2,1)S(1)}, bf16[144,1024]{1,0:T(8,128)(2,1)S(1)}, u32[]{:S(2)}, u32[]{:S(2)}) collective-permute-start(bf16[144,1024]{1,0:T(8,128)(2,1)S(1)} %fusion.34.refs_0_), channel_id=1, source_target_pairs={{0,6},{1,7},{2,0},{3,1},{4,2},{5,3},{6,4},{7,5},{8,14},{9,15},{10,... | collective-permute-start | bytes 884744 | tf_op jit(solution)/shard_map/ppermute | solution.py:311
  12.2 19.0 %collective-permute-start.7 = (bf16[144,1024]{1,0:T(8,128)(2,1)S(1)}, bf16[144,1024]{1,0:T(8,128)(2,1)S(1)}, u32[]{:S(2)}, u32[]{:S(2)}) collective-permute-start(bf16[144,1024]{1,0:T(8,128)(2,1)S(1)} %pad_maximum_fusion.3.refs_8_), channel_id=1, source_target_pairs={{0,16},{8,24},{16,0},{24,8},{1,17},{9,25},{17,1},{25,9},{2,18},{10... | collective-permute-start | bytes 884744 | tf_op jit(solution)/shard_map/ppermute | solution.py:248
  13.8 19.0 %collective-permute-start.3 = (bf16[144,1024]{1,0:T(8,128)(2,1)S(1)}, bf16[144,1024]{1,0:T(8,128)(2,1)}, u32[]{:S(2)}, u32[]{:S(2)}) collective-permute-start(bf16[144,1024]{1,0:T(8,128)(2,1)S(1)} %fusion.34.refs_0_), channel_id=1, source_target_pairs={{0,1},{1,0},{2,3},{3,2},{4,5},{5,4},{6,7},{7,6},{8,9},{9,8},{10,11... | collective-permute-start | bytes 884744 | tf_op jit(solution)/shard_map/ppermute | solution.py:311
  31.2 19.4 %collective-permute-start.6 = (bf16[144,1024]{1,0:T(8,128)(2,1)S(1)}, bf16[144,1024]{1,0:T(8,128)(2,1)S(1)}, u32[]{:S(2)}, u32[]{:S(2)}) collective-permute-start(bf16[144,1024]{1,0:T(8,128)(2,1)S(1)} %collective-permute-done.2.refs_3_), channel_id=1, source_target_pairs={{0,1},{1,0},{2,3},{3,2},{4,5},{5,4},{6,7},{7,6},{8,9},{9,8},{10,11... | collective-permute-start | bytes 884744 | tf_op jit(solution)/shard_map/ppermute | solution.py:311
  59.4 30.3 %collective-permute-start.10 = (bf16[256,1024]{1,0:T(8,128)(2,1)}, bf16[256,1024]{1,0:T(8,128)(2,1)S(1)}, u32[]{:S(2)}, u32[]{:S(2)}) collective-permute-start(bf16[256,1024]{1,0:T(8,128)(2,1)} %get-tuple-element.60), channel_id=1, source_target_pairs={{0,8},{8,0},{16,24},{24,16},{1,9},{9,1},{17,25},{25,17},{2,10},{10... | collective-permute-start | bytes 1572872 | tf_op jit(solution)/shard_map/ppermute | solution.py:248
  64.4 23.1 %collective-permute-start.13 = (bf16[144,1024]{1,0:T(8,128)(2,1)S(1)}, bf16[144,1024]{1,0:T(8,128)(2,1)S(1)}, u32[]{:S(2)}, u32[]{:S(2)}) collective-permute-start(bf16[144,1024]{1,0:T(8,128)(2,1)S(1)} %pad_maximum_fusion.4.refs_0_), channel_id=1, source_target_pairs={{0,4},{1,5},{2,6},{3,7},{4,0},{5,1},{6,2},{7,3},{8,12},{9,13},{10,... | collective-permute-start | bytes 884744 | tf_op jit(solution)/shard_map/ppermute | solution.py:311
  67.8 21.4 %collective-permute-start.14 = (bf16[144,1024]{1,0:T(8,128)(2,1)S(1)}, bf16[144,1024]{1,0:T(8,128)(2,1)S(1)}, u32[]{:S(2)}, u32[]{:S(2)}) collective-permute-start(bf16[144,1024]{1,0:T(8,128)(2,1)S(1)} %pad_maximum_fusion.4.refs_0_), channel_id=1, source_target_pairs={{0,6},{1,7},{2,0},{3,1},{4,2},{5,3},{6,4},{7,5},{8,14},{9,15},{10,... | collective-permute-start | bytes 884744 | tf_op jit(solution)/shard_map/ppermute | solution.py:311
  67.8 28.6 %collective-permute-start.15 = (bf16[144,1024]{1,0:T(8,128)(2,1)S(1)}, bf16[144,1024]{1,0:T(8,128)(2,1)S(1)}, u32[]{:S(2)}, u32[]{:S(2)}) collective-permute-start(bf16[144,1024]{1,0:T(8,128)(2,1)S(1)} %pad_maximum_fusion.4.refs_0_), channel_id=1, source_target_pairs={{0,1},{1,0},{2,3},{3,2},{4,5},{5,4},{6,7},{7,6},{8,9},{9,8},{10,11... | collective-permute-start | bytes 884744 | tf_op jit(solution)/shard_map/ppermute | solution.py:311
  75.2 22.7 %collective-permute-start.16 = (bf16[144,1024]{1,0:T(8,128)(2,1)S(1)}, bf16[144,1024]{1,0:T(8,128)(2,1)S(1)}, u32[]{:S(2)}, u32[]{:S(2)}) collective-permute-start(bf16[144,1024]{1,0:T(8,128)(2,1)S(1)} %collective-permute-done.12.refs_1_), channel_id=1, source_target_pairs={{0,1},{1,0},{2,3},{3,2},{4,5},{5,4},{6,7},{7,6},{8,9},{9,8},{10,11... | collective-permute-start | bytes 884744 | tf_op jit(solution)/shard_map/ppermute | solution.py:311
  89.7 21.6 %collective-permute-start.19 = (bf16[128,1024]{1,0:T(8,128)(2,1)S(1)}, bf16[128,1024]{1,0:T(8,128)(2,1)S(1)}, u32[]{:S(2)}, u32[]{:S(2)}) collective-permute-start(bf16[128,1024]{1,0:T(8,128)(2,1)S(1)} %convert_element_type.250.refs_0_), channel_id=1, source_target_pairs={{0,2},{1,3},{2,4},{3,5},{4,6},{5,7},{6,0},{7,1},{8,10},{9,11},{10,... | collective-permute-start | bytes 786440 | tf_op jit(solution)/shard_map/ppermute | solution.py:311
  111.3 20.0 %collective-permute-start.22 = (bf16[128,1024]{1,0:T(8,128)(2,1)S(1)}, bf16[128,1024]{1,0:T(8,128)(2,1)S(1)}, u32[]{:S(2)}, u32[]{:S(2)}) collective-permute-start(bf16[128,1024]{1,0:T(8,128)(2,1)S(1)} %convert_element_type.250.refs_0_), channel_id=1, source_target_pairs={{0,1},{1,0},{2,3},{3,2},{4,5},{5,4},{6,7},{7,6},{8,9},{9,8},{10,11... | collective-permute-start | bytes 786440 | tf_op jit(solution)/shard_map/ppermute | solution.py:311
  177.0 24.4 %collective-permute-start.57 = (bf16[256,1024]{1,0:T(8,128)(2,1)S(1)}, bf16[256,1024]{1,0:T(8,128)(2,1)S(1)}, u32[]{:S(2)}, u32[]{:S(2)}) collective-permute-start(bf16[256,1024]{1,0:T(8,128)(2,1)S(1)} %convolution_convert_fusion), channel_id=1, source_target_pairs={{0,1},{1,0},{2,3},{3,2},{4,5},{5,4},{6,7},{7,6},{8,9},{9,8},{10,11... | collective-permute-start | bytes 1572872 | tf_op jit(solution)/shard_map/ppermute | solution.py:311
  177.9 34.8 %collective-permute-start.50 = (bf16[256,1024]{1,0:T(8,128)(2,1)S(1)}, bf16[256,1024]{1,0:T(8,128)(2,1)S(1)}, u32[]{:S(2)}, u32[]{:S(2)}) collective-permute-start(bf16[256,1024]{1,0:T(8,128)(2,1)S(1)} %convolution_convert_fusion.3), channel_id=1, source_target_pairs={{0,1},{1,0},{2,3},{3,2},{4,5},{5,4},{6,7},{7,6},{8,9},{9,8},{10,11... | collective-permute-start | bytes 1572872 | tf_op jit(solution)/shard_map/ppermute | solution.py:311
  180.0 43.3 %collective-permute-start.52 = (bf16[256,1024]{1,0:T(8,128)(2,1)S(1)}, bf16[256,1024]{1,0:T(8,128)(2,1)S(1)}, u32[]{:S(2)}, u32[]{:S(2)}) collective-permute-start(bf16[256,1024]{1,0:T(8,128)(2,1)S(1)} %convolution_convert_fusion.2), channel_id=1, source_target_pairs={{0,1},{1,0},{2,3},{3,2},{4,5},{5,4},{6,7},{7,6},{8,9},{9,8},{10,11... | collective-permute-start | bytes 1572872 | tf_op jit(solution)/shard_map/ppermute | solution.py:311
  180.7 51.8 %collective-permute-start.35 = (bf16[128,1024]{1,0:T(8,128)(2,1)S(1)}, bf16[128,1024]{1,0:T(8,128)(2,1)S(1)}, u32[]{:S(2)}, u32[]{:S(2)}) collective-permute-start(bf16[128,1024]{1,0:T(8,128)(2,1)S(1)} %slice.444), channel_id=1, source_target_pairs={{0,16},{8,24},{16,0},{24,8},{1,17},{9,25},{17,1},{25,9},{2,18},{10... | collective-permute-start | bytes 786440 | tf_op jit(solution)/shard_map/ppermute | solution.py:248
  190.7 43.6 %collective-permute-start.56 = (bf16[128,1024]{1,0:T(8,128)(2,1)S(1)}, bf16[128,1024]{1,0:T(8,128)(2,1)S(1)}, u32[]{:S(2)}, u32[]{:S(2)}) collective-permute-start(bf16[128,1024]{1,0:T(8,128)(2,1)S(1)} %slice.441), channel_id=1, source_target_pairs={{0,6},{1,7},{2,0},{3,1},{4,2},{5,3},{6,4},{7,5},{8,14},{9,15},{10,... | collective-permute-start | bytes 786440 | tf_op jit(solution)/shard_map/ppermute | solution.py:311
  201.9 33.2 %collective-permute-start.58 = (bf16[128,1024]{1,0:T(8,128)(2,1)S(1)}, bf16[128,1024]{1,0:T(8,128)(2,1)S(1)}, u32[]{:S(2)}, u32[]{:S(2)}) collective-permute-start(bf16[128,1024]{1,0:T(8,128)(2,1)S(1)} %get-tuple-element.134), channel_id=1, source_target_pairs={{0,4},{1,5},{2,6},{3,7},{4,0},{5,1},{6,2},{7,3},{8,12},{9,13},{10,... | collective-permute-start | bytes 786440 | tf_op jit(solution)/shard_map/ppermute | solution.py:311
  212.6 23.1 %collective-permute-start.59 = (bf16[128,1024]{1,0:T(8,128)(2,1)S(1)}, bf16[128,1024]{1,0:T(8,128)(2,1)S(1)}, u32[]{:S(2)}, u32[]{:S(2)}) collective-permute-start(bf16[128,1024]{1,0:T(8,128)(2,1)S(1)} %get-tuple-element.135), channel_id=1, source_target_pairs={{0,2},{1,3},{2,4},{3,5},{4,6},{5,7},{6,0},{7,1},{8,10},{9,11},{10,... | collective-permute-start | bytes 786440 | tf_op jit(solution)/shard_map/ppermute | solution.py:311
  223.3 19.7 %collective-permute-start.51 = (bf16[128,1024]{1,0:T(8,128)(2,1)S(1)}, bf16[128,1024]{1,0:T(8,128)(2,1)S(1)}, u32[]{:S(2)}, u32[]{:S(2)}) collective-permute-start(bf16[128,1024]{1,0:T(8,128)(2,1)S(1)} %slice.442), channel_id=1, source_target_pairs={{0,6},{1,7},{2,0},{3,1},{4,2},{5,3},{6,4},{7,5},{8,14},{9,15},{10,... | collective-permute-start | bytes 786440 | tf_op jit(solution)/shard_map/ppermute | solution.py:311
  232.6 20.7 %collective-permute-start.53 = (bf16[128,1024]{1,0:T(8,128)(2,1)S(1)}, bf16[128,1024]{1,0:T(8,128)(2,1)S(1)}, u32[]{:S(2)}, u32[]{:S(2)}) collective-permute-start(bf16[128,1024]{1,0:T(8,128)(2,1)S(1)} %get-tuple-element.136), channel_id=1, source_target_pairs={{0,4},{1,5},{2,6},{3,7},{4,0},{5,1},{6,2},{7,3},{8,12},{9,13},{10,... | collective-permute-start | bytes 786440 | tf_op jit(solution)/shard_map/ppermute | solution.py:311
  235.7 19.1 %collective-permute-start.37 = (bf16[144,1024]{1,0:T(8,128)(2,1)S(1)}, bf16[144,1024]{1,0:T(8,128)(2,1)S(1)}, u32[]{:S(2)}, u32[]{:S(2)}) collective-permute-start(bf16[144,1024]{1,0:T(8,128)(2,1)S(1)} %pad_maximum_fusion.5.refs_0_), channel_id=1, source_target_pairs={{0,8},{8,0},{16,24},{24,16},{1,9},{9,1},{17,25},{25,17},{2,10},{10... | collective-permute-start | bytes 884744 | tf_op jit(solution)/shard_map/ppermute | solution.py:248
  267.6 27.8 %collective-permute-start.43 = (bf16[192,1024]{1,0:T(8,128)(2,1)S(1)}, bf16[192,1024]{1,0:T(8,128)(2,1)}, u32[]{:S(2)}, u32[]{:S(2)}) collective-permute-start(bf16[192,1024]{1,0:T(8,128)(2,1)S(1)} %convolution_convert_fusion.4), channel_id=1, source_target_pairs={{0,1},{1,0},{2,3},{3,2},{4,5},{5,4},{6,7},{7,6},{8,9},{9,8},{10,11... | collective-permute-start | bytes 1179656 | tf_op jit(solution)/shard_map/ppermute | solution.py:311
  304.0 19.7 %collective-permute-start.40 = (bf16[128,1024]{1,0:T(8,128)(2,1)S(1)}, bf16[128,1024]{1,0:T(8,128)(2,1)S(1)}, u32[]{:S(2)}, u32[]{:S(2)}) collective-permute-start(bf16[128,1024]{1,0:T(8,128)(2,1)S(1)} %slice.443), channel_id=1, source_target_pairs={{0,16},{8,24},{16,0},{24,8},{1,17},{9,25},{17,1},{25,9},{2,18},{10... | collective-permute-start | bytes 786440 | tf_op jit(solution)/shard_map/ppermute | solution.py:248
  (128 other events, 1897.0 us)
where the time goes:
time: 325 us; the launch traced here: 324 us
  waiting for transfers between devices  157 us (48%)
  starting transfers between devices  93.2 us (29%)
  Pallas kernels  32.8 us (10%)
  other arithmetic  19.6 us (6%)
  matrix products  12.7 us (4%)
  local copies, waits for them, and re-layouts  7.59 us (2%)
    ppermute x40, waiting for transfers between devices, shift(): return lax.ppermute(value, 'rep', pairs)  132 us
    ppermute x40, starting transfers between devices, shift(): return lax.ppermute(value, 'rep', pairs)  85 us
    pallas_call x5, Pallas kernels, call(): pl.pallas_call(kernel, out_shape=[jax.ShapeDtypeStruct(shape, dtype) for...  32.8 us
    ppermute x20, waiting for transfers between devices, swap(): return lax.ppermute(value, 'shard', [(i, i ^ bit) for i in range(groups)])  24.7 us
    dot_general x14, matrix products, dot_on(): lax.dot_general(left_side, right_side, (((left_dim,), (right_dim,)), ((),...  11.3 us
    ppermute x20, starting transfers between devices, swap(): return lax.ppermute(value, 'shard', [(i, i ^ bit) for i in range(groups)])  8.22 us
  transfers between devices with their start and end apart: 60, of which 28 were waited for; matrix products, arithmetic and copies ran while one was open for 7% of the time, Pallas kernels for 2%

commit v1 on v0

--- a/solution.py
+++ b/solution.py
@@ -302,21 +302,24 @@
         aligned = intake.shape[1] % 16 == 0
         head_rows = intake.shape[1] if aligned else HEAD_DIM
 
-        def shift(value, level, amount):
+        sent_as = {}
+
+        def shift(value, level, amount, name):
             pairs = []
             for r in range(replicas):
                 coord = (r // strides[level]) % factors[level]
                 moved = (coord + amount) % factors[level]
                 pairs.append((r, r + (moved - coord) * strides[level]))
+            sent_as[name] = value
             return lax.ppermute(value, "rep", pairs)
 
-        def gather_rep(piece):
-            parts = [piece] + [shift(piece, 0, k) for k in range(1, lead)]
+        def gather_rep(piece, tag):
+            parts = [piece] + [shift(piece, 0, k, f"{tag}_z{k}") for k in range(1, lead)]
             if bulk:
                 return gather_rest({(): jnp.concatenate(parts, axis=0)})
             blocks = list(parts)
             for k in range(1, len(suffixes)):
-                blocks += [shift(v, 1, k) for v in parts]
+                blocks += [shift(v, 1, k, f"{tag}_y{k}_{j}") for j, v in enumerate(parts)]
             return blocks
 
         def gather_rest(blocks):
@@ -324,7 +327,7 @@
                 joined = jnp.concatenate(list(blocks.values()), axis=0)
                 grown = {s + (0,): v for s, v in blocks.items()}
                 for k in range(1, factors[level]):
-                    came = jnp.split(shift(joined, level, k), len(blocks))
+                    came = jnp.split(shift(joined, level, k, "bulk"), len(blocks))
                     grown.update({s + (k,): v for s, v in zip(blocks, came)})
                 blocks = grown
             return [p for s in suffixes for p in jnp.split(blocks[s], lead)]
@@ -350,7 +353,10 @@
             split = split.transpose(2, 0, 1, 3, 4)
             return [[p] for p in split.reshape(len(suffixes), -1, product.shape[1])]
 
-        def scatter_rep(blocks, shared=None, units=None):
+        def wait_for(value, gate):
+            return lax.optimization_barrier((value, *gate))[0] if gate else value
+
+        def scatter_rep(blocks, tag, shared=None, units=None, gates=((), (), ())):
             if bulk:
                 blocks = [[jnp.concatenate(parts, axis=0)] for parts in blocks]
             blocks = dict(zip(suffixes, blocks))
@@ -373,7 +379,8 @@
                         if shared is not None and part == 0:
                             line = jnp.concatenate([units[s + (k,)] for s in merged], axis=1)
                         sent = pack([blocks[s + (k,)][part] for s in merged], line)
-                        came = shift(sent, level, -k).astype(f32)
+                        came = shift(sent, level, -k, f"{tag}_y{k}_{part}")
+                        came = wait_for(came, gates[min(part, 1)]).astype(f32)
                         rows = blocks[next(iter(blocks))][part].shape[0]
                         for i, s in enumerate(merged):
                             merged[s][part] = merged[s][part] + came[i * rows : (i + 1) * rows]
@@ -399,7 +406,8 @@
                 line_total = units[()][:, :size]
             for k in range(1, lead):
                 line = None if shared is None else units[()][:, k * size : (k + 1) * size]
-                came = shift(pack([slot(k)], line), 0, -k).astype(f32)
+                came = shift(pack([slot(k)], line), 0, -k, f"{tag}_z{k}")
+                came = wait_for(came, gates[2]).astype(f32)
                 result = result + came[:rows]
                 if shared is not None:
                     total = total + came[rows : rows + small_rows]
@@ -426,11 +434,17 @@
         out_rows = outlet.shape[0]
         wide_rows = expand.shape[0]
         pieces = gather_rep(
-            jnp.concatenate([intake_low, outlet.astype(bf16), placed, unit_row], axis=0)
-        )
-        placed_group = sum(p[own_rows:].astype(f32) for p in token_parts).astype(bf16)
-        wide_pieces = gather_rep(jnp.concatenate([expand.astype(bf16), placed_group], axis=0))
-        shrink_pieces = gather_rep(shrink.astype(bf16))
+            jnp.concatenate([intake_low, outlet.astype(bf16), placed, unit_row], axis=0), "ga"
+        )
+        placed_group = sum(p[own_rows : own_rows + small_rows].astype(f32) for p in token_parts)
+        placed_group = placed_group.astype(bf16)
+        for level, factor in enumerate(factors):
+            own_sum = placed_group
+            for k in range(1, factor):
+                placed_group = placed_group + shift(own_sum, level, k, f"gs_{level}_{k}")
+        coeffs = placed_group.astype(f32)
+        wide_pieces = gather_rep(expand.astype(bf16), "gb")
+        shrink_pieces = gather_rep(shrink.astype(bf16), "gc")
         unit_cols = offset.shape[0]
         if not aligned:
             at = in_rows + out_rows
@@ -440,13 +454,10 @@
             w_in = order_heads(join(pieces, 0, in_rows), 3)
             w_out = order_heads(join(pieces, in_rows, at), 1)
             pieces = [jnp.concatenate([w_in, w_out, placed_all, line], axis=0)]
-            wide_joined = join(wide_pieces, 0, wide_rows)
-            placed_all = sum(p[wide_rows:].astype(f32) for p in wide_pieces).astype(bf16)
-            wide_pieces = [jnp.concatenate([wide_joined, placed_all], axis=0)]
+            wide_pieces = [join(wide_pieces, 0, wide_rows)]
             shrink_pieces = [join(shrink_pieces, 0, wide_rows)]
             in_rows, out_rows = in_rows * replicas, out_rows * replicas
             wide_rows, unit_cols = wide_rows * replicas, unit_cols * replicas
-        coeffs = sum(p[wide_rows : wide_rows + small_rows].astype(f32) for p in wide_pieces)
         units = wide_rows * len(wide_pieces)
 
         index = lax.broadcasted_iota(jnp.int32, (head_cols, 1), 0)
@@ -551,18 +562,15 @@
             products = [dot_cols(left, right_side) for left in lefts]
             return [products[i * parts : (i + 1) * parts] for i in range(len(suffixes))]
 
-        shrink_grad = scatter_rep(unit_blocks(acts, group_grad))
         grad_inner = scatter_group(near, far)
-        expand_grad = scatter_rep(unit_blocks(backs, group_in))
         grad_mixed = grad_two + grad_inner
         grad_one = norm_back(grad_mixed * (1.0 + coeffs[3]), normed_one, inv_one)
         gain_one = jnp.sum(grad_mixed * normed_one, axis=0)
         shift_one = jnp.sum(grad_mixed, axis=0)
         sums = jnp.stack([gain_one, shift_one, gain_two, shift_two])
         sums = jnp.pad(sums, ((0, extra - sums.shape[0]), (0, 0)))
-        one_parts = gather_group(
-            jnp.concatenate([grad_one.astype(bf16), sums.astype(bf16)], axis=0)
-        )
+        one_sent = jnp.concatenate([grad_one.astype(bf16), sums.astype(bf16)], axis=0)
+        one_parts = gather_group(one_sent)
         group_one, sums, inner_grad, head_sums, far, near = call(
             lambda *refs: attend_back_kernel(head_rows, groups, *refs),
             [
@@ -581,7 +589,6 @@
             scratch=[((head_cols, seq_len), bf16)],
         )
         token_grad = (grad_one + scatter_group(near, far)).astype(bf16)
-        outlet_grad = scatter_rep(by_suffix(attended, group_one, 1, 1))
         bias_rows = lax.dot_general(
             head_sums,
             picks.astype(f32),
@@ -594,8 +601,18 @@
         )
         intake_grad, affine_full, offset_grad = scatter_rep(
             by_suffix(inner_grad, group_tokens, 3, parts),
+            "in",
             shared,
             jnp.split(unit_sums, len(suffixes), axis=1),
+        )
+        late = tuple(sent_as[f"in_z{k}"] for k in range(1, lead))
+        last = (sent_as["in_y1_0"],)
+        shrink_grad = scatter_rep(
+            unit_blocks(acts, group_grad), "sh", gates=((one_sent,), (one_sent,), late)
+        )
+        expand_grad = scatter_rep(unit_blocks(backs, group_in), "ex", gates=(last, (far,), late))
+        outlet_grad = scatter_rep(
+            by_suffix(attended, group_one, 1, 1), "ou", gates=(last, last, late)
         )
         intake_grad = intake_grad.reshape(intake.shape)
         offset_grad = offset_grad.reshape(offset.shape)

time: 325 us -> 312 us (0.960)
  waiting for transfers between devices: 157 us -> 134 us
  starting transfers between devices: 93.2 us -> 96.9 us
    ppermute x40 -> x44, waiting for transfers between devices: 132 us -> 108 us  [shift(): return lax.ppermute(value, 'rep', pairs)]
    ppermute x20, starting transfers between devices: 8.22 us -> 12.5 us  [swap(): return lax.ppermute(value, 'shard', [(i, i ^ bit) for i in range(groups)])]
    ppermute x40 -> x44, starting transfers between devices: 85 us -> 84.4 us  [shift(): return lax.ppermute(value, 'rep', pairs)]
  transfers between devices with their start and end apart: 60 -> 64, of which waited for: 28 -> 25; matrix products, arithmetic and copies ran while one was open for 7% -> 11% of each run, Pallas kernels for 2% -> 5%
where the time goes in v1:
time: 312 us; the launch traced here: 311 us
  waiting for transfers between devices  134 us (43%)
  starting transfers between devices  96.9 us (31%)
  Pallas kernels  32.8 us (11%)
  other arithmetic  20.6 us (7%)
  matrix products  14.5 us (5%)
  local copies, waits for them, and re-layouts  10.1 us (3%)
    ppermute x44, waiting for transfers between devices, shift(): return lax.ppermute(value, 'rep', pairs)  108 us
    ppermute x44, starting transfers between devices, shift(): return lax.ppermute(value, 'rep', pairs)  84.4 us
    pallas_call x5, Pallas kernels, call(): pl.pallas_call(kernel, out_shape=[jax.ShapeDtypeStruct(shape, dtype) for...  32.8 us
    ppermute x20, waiting for transfers between devices, swap(): return lax.ppermute(value, 'shard', [(i, i ^ bit) for i in range(groups)])  25.9 us
    dot_general x14, matrix products, dot_on(): lax.dot_general(left_side, right_side, (((left_dim,), (right_dim,)), ((),...  13.1 us
    ppermute x20, starting transfers between devices, swap(): return lax.ppermute(value, 'shard', [(i, i ^ bit) for i in range(groups)])  12.5 us
    sub x6, other arithmetic, adamw_step(): weight - lr_rate * (fixed_mom / (jnp.sqrt(fixed_var) + adam_eps) + weight...  7.44 us
  transfers between devices with their start and end apart: 64, of which 25 were waited for; matrix products, arithmetic and copies ran while one was open for 11% of the time, Pallas kernels for 5%

profile of v1, /device:TPU:0, one launch (start us, length us, event | category | flops | bytes accessed | tf_op | source)
XLA Modules:
  0.0 310.9 jit_solution(10782377303929097243)
XLA Ops:
  18.3 11.8 %collective-permute-done.1.refs_2_ = bf16[144,1024]{1,0:T(8,128)(2,1)S(1)} collective-permute-done((bf16[144,1024]{1,0:T(8,128)(2,1)S(1)}, bf16[144,1024]{1,0:T(8,128)(2,1)S(1)}, u32[]{:S(2)}, u32[]{:S(2)}) %collective-permute-start.1) | collective-permute-done | bytes 294944 | tf_op jit(solution)/shard_map/ppermute | solution.py:314
  34.7 5.3 %collective-permute-done.4.refs_5_ = bf16[144,1024]{1,0:T(8,128)(2,1)S(1)} collective-permute-done((bf16[144,1024]{1,0:T(8,128)(2,1)S(1)}, bf16[144,1024]{1,0:T(8,128)(2,1)S(1)}, u32[]{:S(2)}, u32[]{:S(2)}) %collective-permute-start.4) | collective-permute-done | bytes 294944 | tf_op jit(solution)/shard_map/ppermute | solution.py:314
  40.0 6.3 %collective-permute-done.5.refs_6_ = bf16[144,1024]{1,0:T(8,128)(2,1)S(1)} collective-permute-done((bf16[144,1024]{1,0:T(8,128)(2,1)S(1)}, bf16[144,1024]{1,0:T(8,128)(2,1)S(1)}, u32[]{:S(2)}, u32[]{:S(2)}) %collective-permute-start.5) | collective-permute-done | bytes 294944 | tf_op jit(solution)/shard_map/ppermute | solution.py:314
  46.3 5.3 %collective-permute-done.6.refs_7_ = bf16[144,1024]{1,0:T(8,128)(2,1)S(1)} collective-permute-done((bf16[144,1024]{1,0:T(8,128)(2,1)S(1)}, bf16[144,1024]{1,0:T(8,128)(2,1)S(1)}, u32[]{:S(2)}, u32[]{:S(2)}) %collective-permute-start.6) | collective-permute-done | bytes 294944 | tf_op jit(solution)/shard_map/ppermute | solution.py:314
  53.0 7.3 %shard_map.404 = (bf16[768,1024]{1,0:T(8,128)(2,1)}, bf16[256,1024]{1,0:T(8,128)(2,1)}, bf16[512,1024]{1,0:T(8,128)(2,1)}, bf16[768,512]{1,0:T(8,128)(2,1)}, bf1...) custom-call(bf16[144,1024]{1,0:T(8,128)(2,1)} %copy-done.14, ...), custom_call_target="tpu_custom_call" | custom-call | tf_op jit(solution)/shard_map/pallas_call | solution.py:491
  75.7 5.2 %collective-permute-done.15 = bf16[8,1024]{1,0:T(8,128)(2,1)S(1)} collective-permute-done((bf16[8,1024]{1,0:T(8,128)(2,1)S(1)}, bf16[8,1024]{1,0:T(8,128)(2,1)S(1)}, u32[]{:S(2)}, u32[]{:S(2)}) %collective-permute-start.15) | collective-permute-done | bytes 16416 | tf_op jit(solution)/shard_map/ppermute | solution.py:314
  82.4 4.9 %collective-permute-done.11 = bf16[128,1024]{1,0:T(8,128)(2,1)S(1)} collective-permute-done((bf16[128,1024]{1,0:T(8,128)(2,1)S(1)}, bf16[128,1024]{1,0:T(8,128)(2,1)S(1)}, u32[]{:S(2)}, u32[]{:S(2)}) %collective-permute-start.11) | collective-permute-done | bytes 262176 | tf_op jit(solution)/shard_map/ppermute | solution.py:248
  91.0 7.9 %collective-permute-start.18 = (bf16[128,1024]{1,0:T(8,128)(2,1)S(1)}, bf16[128,1024]{1,0:T(8,128)(2,1)S(1)}, u32[]{:S(2)}, u32[]{:S(2)}) collective-permute-start(bf16[128,1024]{1,0:T(8,128)(2,1)S(1)} %convert_element_type.221.refs_0_), channel_id=1, source_target_pairs={{0,6},{1,7},{2,0},{3,1},{4,2},{5,3},{6,4},{7,5},{8,14},{9,15},{10,... | collective-permute-start | bytes 786440 | tf_op jit(solution)/shard_map/ppermute | solution.py:314
  102.6 9.9 %collective-permute-done.17.refs_2_ = bf16[128,1024]{1,0:T(8,128)(2,1)S(1)} collective-permute-done((bf16[128,1024]{1,0:T(8,128)(2,1)S(1)}, bf16[128,1024]{1,0:T(8,128)(2,1)S(1)}, u32[]{:S(2)}, u32[]{:S(2)}) %collective-permute-start.17) | collective-permute-done | bytes 262176 | tf_op jit(solution)/shard_map/ppermute | solution.py:314
  116.5 5.2 %collective-permute-done.29.refs_7_ = bf16[128,1024]{1,0:T(8,128)(2,1)S(1)} collective-permute-done((bf16[128,1024]{1,0:T(8,128)(2,1)S(1)}, bf16[128,1024]{1,0:T(8,128)(2,1)S(1)}, u32[]{:S(2)}, u32[]{:S(2)}) %collective-permute-start.29) | collective-permute-done | bytes 262176 | tf_op jit(solution)/shard_map/ppermute | solution.py:314
  124.8 5.5 %shard_map.405 = (bf16[1024,1024]{1,0:T(8,128)(2,1)}, bf16[512,1024]{1,0:T(8,128)(2,1)}, f32[512,1024]{1,0:T(8,128)}, bf16[512,256]{1,0:T(8,128)(2,1)}, bf16[512...) custom-call(bf16[128,1024]{1,0:T(8,128)(2,1)} %copy-done.18, bf16[128,1024]{1,0:T(8,128)(2,1)} %copy-done.49, ...), custom_call_target="tpu_custom_call" | custom-call | tf_op jit(solution)/shard_map/pallas_call | solution.py:491
  133.0 5.6 %collective-permute-done.21.refs_6_ = bf16[128,1024]{1,0:T(8,128)(2,1)} collective-permute-done((bf16[128,1024]{1,0:T(8,128)(2,1)S(1)}, bf16[128,1024]{1,0:T(8,128)(2,1)}, u32[]{:S(2)}, u32[]{:S(2)}) %collective-permute-start.21) | collective-permute-done | bytes 262176 | tf_op jit(solution)/shard_map/ppermute | solution.py:314
  138.6 4.6 %collective-permute-done.22.refs_7_ = bf16[128,1024]{1,0:T(8,128)(2,1)} collective-permute-done((bf16[128,1024]{1,0:T(8,128)(2,1)S(1)}, bf16[128,1024]{1,0:T(8,128)(2,1)}, u32[]{:S(2)}, u32[]{:S(2)}) %collective-permute-start.22) | collective-permute-done | bytes 262176 | tf_op jit(solution)/shard_map/ppermute | solution.py:314
  152.4 6.9 %collective-permute-done.34 = bf16[128,1024]{1,0:T(8,128)(2,1)S(1)} collective-permute-done((bf16[128,1024]{1,0:T(8,128)(2,1)S(1)}, bf16[128,1024]{1,0:T(8,128)(2,1)S(1)}, u32[]{:S(2)}, u32[]{:S(2)}) %collective-permute-start.34) | collective-permute-done | bytes 262176 | tf_op jit(solution)/shard_map/ppermute | solution.py:248
  161.9 6.0 %collective-permute-done.35.refs_1_ = bf16[128,1024]{1,0:T(8,128)(2,1)S(1)} collective-permute-done((bf16[128,1024]{1,0:T(8,128)(2,1)S(1)}, bf16[128,1024]{1,0:T(8,128)(2,1)S(1)}, u32[]{:S(2)}, u32[]{:S(2)}) %collective-permute-start.35) | collective-permute-done | bytes 262176 | tf_op jit(solution)/shard_map/ppermute | solution.py:248
  170.2 6.8 %shard_map.407 = (bf16[512,1024]{1,0:T(8,128)(2,1)}, f32[1,1024]{1,0:T(1,128)}, f32[1,1024]{1,0:T(1,128)}, bf16[256,1024]{1,0:T(8,128)(2,1)}, f32[256,1024]{1,0:...) custom-call(bf16[128,1024]{1,0:T(8,128)(2,1)} %copy-done.25, ...), custom_call_target="tpu_custom_call" | custom-call | tf_op jit(solution)/shard_map/pallas_call | solution.py:491
  189.9 4.5 %collective-permute-done.39 = bf16[128,1024]{1,0:T(8,128)(2,1)S(1)} collective-permute-done((bf16[128,1024]{1,0:T(8,128)(2,1)S(1)}, bf16[128,1024]{1,0:T(8,128)(2,1)S(1)}, u32[]{:S(2)}, u32[]{:S(2)}) %collective-permute-start.39) | collective-permute-done | bytes 262176 | tf_op jit(solution)/shard_map/ppermute | solution.py:248
  199.6 6.3 %collective-permute-done.61 = bf16[256,1024]{1,0:T(8,128)(2,1)S(1)} collective-permute-done((bf16[256,1024]{1,0:T(8,128)(2,1)S(1)}, bf16[256,1024]{1,0:T(8,128)(2,1)S(1)}, u32[]{:S(2)}, u32[]{:S(2)}) %collective-permute-start.61) | collective-permute-done | bytes 524320 | tf_op jit(solution)/shard_map/ppermute | solution.py:314
  205.8 6.0 %collective-permute-start.60 = (bf16[128,1024]{1,0:T(8,128)(2,1)}, bf16[128,1024]{1,0:T(8,128)(2,1)}, u32[]{:S(2)}, u32[]{:S(2)}) collective-permute-start(bf16[128,1024]{1,0:T(8,128)(2,1)} %slice.394), channel_id=1, source_target_pairs={{0,6},{1,7},{2,0},{3,1},{4,2},{5,3},{6,4},{7,5},{8,14},{9,15},{10,... | collective-permute-start | bytes 786440 | tf_op jit(solution)/shard_map/ppermute | solution.py:314
  215.6 9.0 %shard_map.408 = (bf16[512,1024]{1,0:T(8,128)(2,1)}, f32[16,1024]{1,0:T(8,128)}, bf16[768,512]{1,0:T(8,128)(2,1)}, f32[256,2]{1,0:T(8,128)}, bf16[256,1024]{1,0:T(8,128)(2,1)}, /*index=5*/f32[256,1024]{1,0:T(8,128)}) custom-call(bf16[144,1024]{1,0:T(8,128)(2,1)} %copy-done.13, bf16[144,1024]{1,0:T(8,128)(2,1)} %copy-done.42, bf16[144,1024]{1,0:T(8,128)(2,1)} %copy-done.44, ...), custom_call_target="tpu_custom_call" | custom-call | tf_op jit(solution)/shard_map/pallas_call | solution.py:491
  235.3 11.4 %collective-permute-done.50 = bf16[128,1024]{1,0:T(8,128)(2,1)S(1)} collective-permute-done((bf16[128,1024]{1,0:T(8,128)(2,1)S(1)}, bf16[128,1024]{1,0:T(8,128)(2,1)S(1)}, u32[]{:S(2)}, u32[]{:S(2)}) %collective-permute-start.50) | collective-permute-done | bytes 262176 | tf_op jit(solution)/shard_map/ppermute | solution.py:314
  248.7 8.4 %collective-permute-done.47 = bf16[192,1024]{1,0:T(8,128)(2,1)S(1)} collective-permute-done((bf16[192,1024]{1,0:T(8,128)(2,1)S(1)}, bf16[192,1024]{1,0:T(8,128)(2,1)S(1)}, u32[]{:S(2)}, u32[]{:S(2)}) %collective-permute-start.47) | collective-permute-done | bytes 393248 | tf_op jit(solution)/shard_map/ppermute | solution.py:314
  266.3 15.9 %collective-permute-start.53 = (bf16[32,1024]{1,0:T(8,128)(2,1)S(1)}, bf16[32,1024]{1,0:T(8,128)(2,1)S(1)}, u32[]{:S(2)}, u32[]{:S(2)}) collective-permute-start(bf16[32,1024]{1,0:T(8,128)(2,1)S(1)} %get-tuple-element.169), channel_id=1, source_target_pairs={{0,2},{1,3},{2,4},{3,5},{4,6},{5,7},{6,0},{7,1},{8,10},{9,11},{10,... | collective-permute-start | bytes 196616 | tf_op jit(solution)/shard_map/ppermute | solution.py:314
  295.6 11.7 %collective-permute-done.48 = bf16[112,1024]{1,0:T(8,128)(2,1)S(1)} collective-permute-done((bf16[112,1024]{1,0:T(8,128)(2,1)S(1)}, bf16[112,1024]{1,0:T(8,128)(2,1)S(1)}, u32[]{:S(2)}, u32[]{:S(2)}) %collective-permute-start.48) | collective-permute-done | bytes 229408 | tf_op jit(solution)/shard_map/ppermute | solution.py:314
  (367 shorter events, 131.2 us)
Async XLA Ops:
  8.3 21.8 %collective-permute-start.1 = (bf16[144,1024]{1,0:T(8,128)(2,1)S(1)}, bf16[144,1024]{1,0:T(8,128)(2,1)S(1)}, u32[]{:S(2)}, u32[]{:S(2)}) collective-permute-start(bf16[144,1024]{1,0:T(8,128)(2,1)S(1)} %get-tuple-element.182.refs_0_), channel_id=1, source_target_pairs={{0,4},{1,5},{2,6},{3,7},{4,0},{5,1},{6,2},{7,3},{8,12},{9,13},{10,... | collective-permute-start | bytes 884744 | tf_op jit(solution)/shard_map/ppermute | solution.py:314
  10.9 20.7 %collective-permute-start.2 = (bf16[144,1024]{1,0:T(8,128)(2,1)S(1)}, bf16[144,1024]{1,0:T(8,128)(2,1)S(1)}, u32[]{:S(2)}, u32[]{:S(2)}) collective-permute-start(bf16[144,1024]{1,0:T(8,128)(2,1)S(1)} %get-tuple-element.182.refs_0_), channel_id=1, source_target_pairs={{0,6},{1,7},{2,0},{3,1},{4,2},{5,3},{6,4},{7,5},{8,14},{9,15},{10,... | collective-permute-start | bytes 884744 | tf_op jit(solution)/shard_map/ppermute | solution.py:314
  12.1 20.0 %collective-permute-start.7 = (bf16[144,1024]{1,0:T(8,128)(2,1)S(1)}, bf16[144,1024]{1,0:T(8,128)(2,1)S(1)}, u32[]{:S(2)}, u32[]{:S(2)}) collective-permute-start(bf16[144,1024]{1,0:T(8,128)(2,1)S(1)} %get-tuple-element.183.refs_8_), channel_id=1, source_target_pairs={{0,16},{8,24},{16,0},{24,8},{1,17},{9,25},{17,1},{25,9},{2,18},{10... | collective-permute-start | bytes 884744 | tf_op jit(solution)/shard_map/ppermute | solution.py:248
  13.6 20.0 %collective-permute-start.3 = (bf16[144,1024]{1,0:T(8,128)(2,1)S(1)}, bf16[144,1024]{1,0:T(8,128)(2,1)}, u32[]{:S(2)}, u32[]{:S(2)}) collective-permute-start(bf16[144,1024]{1,0:T(8,128)(2,1)S(1)} %get-tuple-element.182.refs_0_), channel_id=1, source_target_pairs={{0,1},{1,0},{2,3},{3,2},{4,5},{5,4},{6,7},{7,6},{8,9},{9,8},{10,11... | collective-permute-start | bytes 884744 | tf_op jit(solution)/shard_map/ppermute | solution.py:314
  68.7 19.6 %collective-permute-start.23 = (bf16[128,1024]{1,0:T(8,128)(2,1)S(1)}, bf16[128,1024]{1,0:T(8,128)(2,1)S(1)}, u32[]{:S(2)}, u32[]{:S(2)}) collective-permute-start(bf16[128,1024]{1,0:T(8,128)(2,1)S(1)} %convert_element_type.222.refs_0_), channel_id=1, source_target_pairs={{0,2},{1,3},{2,4},{3,5},{4,6},{5,7},{6,0},{7,1},{8,10},{9,11},{10,... | collective-permute-start | bytes 786440 | tf_op jit(solution)/shard_map/ppermute | solution.py:314
  70.9 20.1 %collective-permute-start.24 = (bf16[128,1024]{1,0:T(8,128)(2,1)S(1)}, bf16[128,1024]{1,0:T(8,128)(2,1)S(1)}, u32[]{:S(2)}, u32[]{:S(2)}) collective-permute-start(bf16[128,1024]{1,0:T(8,128)(2,1)S(1)} %convert_element_type.222.refs_0_), channel_id=1, source_target_pairs={{0,4},{1,5},{2,6},{3,7},{4,0},{5,1},{6,2},{7,3},{8,12},{9,13},{10,... | collective-permute-start | bytes 786440 | tf_op jit(solution)/shard_map/ppermute | solution.py:314
  71.0 28.1 %collective-permute-start.25 = (bf16[128,1024]{1,0:T(8,128)(2,1)S(1)}, bf16[128,1024]{1,0:T(8,128)(2,1)S(1)}, u32[]{:S(2)}, u32[]{:S(2)}) collective-permute-start(bf16[128,1024]{1,0:T(8,128)(2,1)S(1)} %convert_element_type.222.refs_0_), channel_id=1, source_target_pairs={{0,6},{1,7},{2,0},{3,1},{4,2},{5,3},{6,4},{7,5},{8,14},{9,15},{10,... | collective-permute-start | bytes 786440 | tf_op jit(solution)/shard_map/ppermute | solution.py:314
  73.4 27.4 %collective-permute-start.26 = (bf16[128,1024]{1,0:T(8,128)(2,1)S(1)}, bf16[128,1024]{1,0:T(8,128)(2,1)S(1)}, u32[]{:S(2)}, u32[]{:S(2)}) collective-permute-start(bf16[128,1024]{1,0:T(8,128)(2,1)S(1)} %convert_element_type.222.refs_0_), channel_id=1, source_target_pairs={{0,1},{1,0},{2,3},{3,2},{4,5},{5,4},{6,7},{7,6},{8,9},{9,8},{10,11... | collective-permute-start | bytes 786440 | tf_op jit(solution)/shard_map/ppermute | solution.py:314
  88.3 24.2 %collective-permute-start.17 = (bf16[128,1024]{1,0:T(8,128)(2,1)S(1)}, bf16[128,1024]{1,0:T(8,128)(2,1)S(1)}, u32[]{:S(2)}, u32[]{:S(2)}) collective-permute-start(bf16[128,1024]{1,0:T(8,128)(2,1)S(1)} %convert_element_type.221.refs_0_), channel_id=1, source_target_pairs={{0,4},{1,5},{2,6},{3,7},{4,0},{5,1},{6,2},{7,3},{8,12},{9,13},{10,... | collective-permute-start | bytes 786440 | tf_op jit(solution)/shard_map/ppermute | solution.py:314
  91.0 23.2 %collective-permute-start.18 = (bf16[128,1024]{1,0:T(8,128)(2,1)S(1)}, bf16[128,1024]{1,0:T(8,128)(2,1)S(1)}, u32[]{:S(2)}, u32[]{:S(2)}) collective-permute-start(bf16[128,1024]{1,0:T(8,128)(2,1)S(1)} %convert_element_type.221.refs_0_), channel_id=1, source_target_pairs={{0,6},{1,7},{2,0},{3,1},{4,2},{5,3},{6,4},{7,5},{8,14},{9,15},{10,... | collective-permute-start | bytes 786440 | tf_op jit(solution)/shard_map/ppermute | solution.py:314
  123.3 19.9 %collective-permute-start.22 = (bf16[128,1024]{1,0:T(8,128)(2,1)S(1)}, bf16[128,1024]{1,0:T(8,128)(2,1)}, u32[]{:S(2)}, u32[]{:S(2)}) collective-permute-start(bf16[128,1024]{1,0:T(8,128)(2,1)S(1)} %collective-permute-done.18.refs_3_), channel_id=1, source_target_pairs={{0,1},{1,0},{2,3},{3,2},{4,5},{5,4},{6,7},{7,6},{8,9},{9,8},{10,11... | collective-permute-start | bytes 786440 | tf_op jit(solution)/shard_map/ppermute | solution.py:314
  183.1 22.7 %collective-permute-start.61 = (bf16[256,1024]{1,0:T(8,128)(2,1)S(1)}, bf16[256,1024]{1,0:T(8,128)(2,1)S(1)}, u32[]{:S(2)}, u32[]{:S(2)}) collective-permute-start(bf16[256,1024]{1,0:T(8,128)(2,1)S(1)} %convolution_convert_fusion), channel_id=1, source_target_pairs={{0,1},{1,0},{2,3},{3,2},{4,5},{5,4},{6,7},{7,6},{8,9},{9,8},{10,11... | collective-permute-start | bytes 1572872 | tf_op jit(solution)/shard_map/ppermute | solution.py:314
  184.9 44.2 %collective-permute-start.54 = (bf16[256,1024]{1,0:T(8,128)(2,1)}, bf16[256,1024]{1,0:T(8,128)(2,1)}, u32[]{:S(2)}, u32[]{:S(2)}) collective-permute-start(bf16[256,1024]{1,0:T(8,128)(2,1)} %convolution_convert_fusion.3), channel_id=1, source_target_pairs={{0,1},{1,0},{2,3},{3,2},{4,5},{5,4},{6,7},{7,6},{8,9},{9,8},{10,11... | collective-permute-start | bytes 1572872 | tf_op jit(solution)/shard_map/ppermute | solution.py:314
  189.5 42.9 %collective-permute-start.56 = (bf16[256,1024]{1,0:T(8,128)(2,1)}, bf16[256,1024]{1,0:T(8,128)(2,1)}, u32[]{:S(2)}, u32[]{:S(2)}) collective-permute-start(bf16[256,1024]{1,0:T(8,128)(2,1)} %convolution_convert_fusion.2), channel_id=1, source_target_pairs={{0,1},{1,0},{2,3},{3,2},{4,5},{5,4},{6,7},{7,6},{8,9},{9,8},{10,11... | collective-permute-start | bytes 1572872 | tf_op jit(solution)/shard_map/ppermute | solution.py:314
  205.8 55.7 %collective-permute-start.60 = (bf16[128,1024]{1,0:T(8,128)(2,1)}, bf16[128,1024]{1,0:T(8,128)(2,1)}, u32[]{:S(2)}, u32[]{:S(2)}) collective-permute-start(bf16[128,1024]{1,0:T(8,128)(2,1)} %slice.394), channel_id=1, source_target_pairs={{0,6},{1,7},{2,0},{3,1},{4,2},{5,3},{6,4},{7,5},{8,14},{9,15},{10,... | collective-permute-start | bytes 786440 | tf_op jit(solution)/shard_map/ppermute | solution.py:314
  213.1 48.5 %collective-permute-start.62 = (bf16[128,1024]{1,0:T(8,128)(2,1)}, bf16[128,1024]{1,0:T(8,128)(2,1)}, u32[]{:S(2)}, u32[]{:S(2)}) collective-permute-start(bf16[128,1024]{1,0:T(8,128)(2,1)} %get-tuple-element.162), channel_id=1, source_target_pairs={{0,4},{1,5},{2,6},{3,7},{4,0},{5,1},{6,2},{7,3},{8,12},{9,13},{10,... | collective-permute-start | bytes 786440 | tf_op jit(solution)/shard_map/ppermute | solution.py:314
  214.8 50.6 %collective-permute-start.63 = (bf16[128,1024]{1,0:T(8,128)(2,1)}, bf16[128,1024]{1,0:T(8,128)(2,1)}, u32[]{:S(2)}, u32[]{:S(2)}) collective-permute-start(bf16[128,1024]{1,0:T(8,128)(2,1)} %get-tuple-element.163), channel_id=1, source_target_pairs={{0,2},{1,3},{2,4},{3,5},{4,6},{5,7},{6,0},{7,1},{8,10},{9,11},{10,... | collective-permute-start | bytes 786440 | tf_op jit(solution)/shard_map/ppermute | solution.py:314
  229.1 31.0 %collective-permute-start.45 = (bf16[208,1024]{1,0:T(8,128)(2,1)S(1)}, bf16[208,1024]{1,0:T(8,128)(2,1)S(1)}, u32[]{:S(2)}, u32[]{:S(2)}) collective-permute-start(bf16[208,1024]{1,0:T(8,128)(2,1)S(1)} %fusion.33), channel_id=1, source_target_pairs={{0,1},{1,0},{2,3},{3,2},{4,5},{5,4},{6,7},{7,6},{8,9},{9,8},{10,11... | collective-permute-start | bytes 1277960 | tf_op jit(solution)/shard_map/ppermute | solution.py:314
  260.1 26.2 %collective-permute-start.57 = (bf16[128,1024]{1,0:T(8,128)(2,1)S(1)}, bf16[128,1024]{1,0:T(8,128)(2,1)S(1)}, u32[]{:S(2)}, u32[]{:S(2)}) collective-permute-start(bf16[128,1024]{1,0:T(8,128)(2,1)S(1)} %get-tuple-element.164), channel_id=1, source_target_pairs={{0,4},{1,5},{2,6},{3,7},{4,0},{5,1},{6,2},{7,3},{8,12},{9,13},{10,... | collective-permute-start | bytes 786440 | tf_op jit(solution)/shard_map/ppermute | solution.py:314
  261.5 24.7 %collective-permute-start.58 = (bf16[128,1024]{1,0:T(8,128)(2,1)S(1)}, bf16[128,1024]{1,0:T(8,128)(2,1)S(1)}, u32[]{:S(2)}, u32[]{:S(2)}) collective-permute-start(bf16[128,1024]{1,0:T(8,128)(2,1)S(1)} %get-tuple-element.165), channel_id=1, source_target_pairs={{0,2},{1,3},{2,4},{3,5},{4,6},{5,7},{6,0},{7,1},{8,10},{9,11},{10,... | collective-permute-start | bytes 786440 | tf_op jit(solution)/shard_map/ppermute | solution.py:314
  261.6 24.7 %collective-permute-start.51 = (bf16[32,1024]{1,0:T(8,128)(2,1)S(1)}, bf16[32,1024]{1,0:T(8,128)(2,1)S(1)}, u32[]{:S(2)}, u32[]{:S(2)}) collective-permute-start(bf16[32,1024]{1,0:T(8,128)(2,1)S(1)} %get-tuple-element.168), channel_id=1, source_target_pairs={{0,6},{1,7},{2,0},{3,1},{4,2},{5,3},{6,4},{7,5},{8,14},{9,15},{10,... | collective-permute-start | bytes 196616 | tf_op jit(solution)/shard_map/ppermute | solution.py:314
  265.4 22.7 %collective-permute-start.52 = (bf16[32,1024]{1,0:T(8,128)(2,1)S(1)}, bf16[32,1024]{1,0:T(8,128)(2,1)S(1)}, u32[]{:S(2)}, u32[]{:S(2)}) collective-permute-start(bf16[32,1024]{1,0:T(8,128)(2,1)S(1)} %get-tuple-element.170), channel_id=1, source_target_pairs={{0,4},{1,5},{2,6},{3,7},{4,0},{5,1},{6,2},{7,3},{8,12},{9,13},{10,... | collective-permute-start | bytes 196616 | tf_op jit(solution)/shard_map/ppermute | solution.py:314
  266.3 22.4 %collective-permute-start.53 = (bf16[32,1024]{1,0:T(8,128)(2,1)S(1)}, bf16[32,1024]{1,0:T(8,128)(2,1)S(1)}, u32[]{:S(2)}, u32[]{:S(2)}) collective-permute-start(bf16[32,1024]{1,0:T(8,128)(2,1)S(1)} %get-tuple-element.169), channel_id=1, source_target_pairs={{0,2},{1,3},{2,4},{3,5},{4,6},{5,7},{6,0},{7,1},{8,10},{9,11},{10,... | collective-permute-start | bytes 196616 | tf_op jit(solution)/shard_map/ppermute | solution.py:314
  286.3 21.0 %collective-permute-start.48 = (bf16[112,1024]{1,0:T(8,128)(2,1)S(1)}, bf16[112,1024]{1,0:T(8,128)(2,1)S(1)}, u32[]{:S(2)}, u32[]{:S(2)}) collective-permute-start(bf16[112,1024]{1,0:T(8,128)(2,1)S(1)} %get-tuple-element.180), channel_id=1, source_target_pairs={{0,4},{1,5},{2,6},{3,7},{4,0},{5,1},{6,2},{7,3},{8,12},{9,13},{10,... | collective-permute-start | bytes 688136 | tf_op jit(solution)/shard_map/ppermute | solution.py:314
  (121 other events, 1590.4 us)
